TPU v7x, 512 devices: a whole 4x4x16 slice. The times are simulated.
512 devices in a mesh: cfg: 2 (over core), blk: 64 (over z, x), req: 4 (over y).
Axes of the slice: x: 4, y: 4, z: 16, core: 2. Of those that a mesh axis runs over, the one named last changes fastest.
Arguments:
- residual: bfloat16 [2, 16, 2048], P('cfg'), may hold values from -6 to 6
- queries: bfloat16 [2, 16, 4096], P('cfg', 'req'), may hold values from -80 to 80
- new_entries: bfloat16 [2, 16, 2, 2048], P('cfg', 'req'), may hold values from -6 to 6
- key_cache: bfloat16 [2, 16, 3072, 2048], P('cfg', 'req', 'blk'), may hold values from -6 to 6
- value_cache: bfloat16 [2, 16, 3072, 2048], P('cfg', 'req', 'blk'), may hold values from -8 to 8
- lengths: int32 [2, 16], P('cfg', 'req'), may hold values from 2 to 3072, as said below
- attention_ids: int32 [16, 2], replicated, may hold values from 0 to 7, all different within a row
- expert_ids: int32 [16, 2], replicated, may hold values from 0 to 7, all different within a row
- attention_router: bfloat16 [2048, 8], replicated, may hold values from -0.125 to 0.125
- expert_router: bfloat16 [2048, 8], replicated, may hold values from -0.125 to 0.125
- attention_output: bfloat16 [16384, 2048], P(('blk', 'req')), may hold values from -0.125 to 0.125
- expert_gain: bfloat16 [2048], replicated, may hold values from 0.25 to 1.75
- expert_gate: bfloat16 [45056, 2048], P(('blk', 'req')), may hold values from -0.125 to 0.125
- expert_up: bfloat16 [45056, 2048], P(('blk', 'req')), may hold values from -0.125 to 0.125
- expert_down: bfloat16 [45056, 2048], P(('blk', 'req')), may hold values from -0.078125 to 0.078125
- final_gain: bfloat16 [2048], replicated, may hold values from 0.25 to 1.75
- unembedding: bfloat16 [32000, 2048], P(('blk', 'req')), may hold values from -0.125 to 0.125
- tenant_sizes: int32 [4], replicated, may hold values from 1 to 8, 16 in all
- guidance: int32 [4], replicated, may hold values from 2 to 16
Outputs:
- guided: float32 [16, 32000], P('cfg', ('blk', 'req'))
Inputs may be any that keep to these rules, and one draw needn't show every extreme that they name: lengths[0, i] lies from 1536 to 3072 and lengths[0, 0] = 3072; lengths[1, i] lies from 2 to 768 and lengths[1, 0] = 768. `tenant_sizes`: the sizes sum to 16; the largest is exactly 8. `attention_ids`: the ids of one request differ. `expert_ids`: the ids of one request differ.
All inputs are finite; a program needn't handle non-finite values.
Results may differ from a plain program's by a relative error of at most 0.017.
Values may be sent and summed in bfloat16 or wider, within the bound.
No kernel may reach another device: no remote copies, remote signals or barrier semaphores. Data moves between devices by JAX's collectives and lax.ppermute only.
A program may use at most 64 MiB of HBM per device.

v0:
```python
import math

import jax
import jax.numpy as jnp
from jax import lax
from jax.sharding import PartitionSpec as P

H = 16
HD = 128
FF = 5632
TOPK = 2


EPS = 1e-05


def joined(shard, axis, combine):
    everything = jax.tree.map(
        lambda part, kind: lax.all_gather(part.astype(kind), axis),
        shard,
        (jnp.bfloat16, jnp.bfloat16, jnp.bfloat16),
    )

    def take(k):
        return jax.tree.map(lambda part, own: part[k].astype(own.dtype), everything, shard)

    return lax.fori_loop(
        1, lax.axis_size(axis), lambda k, so_far: combine(so_far, take(k)), take(0)
    )


def swapped(value, axis, bit):
    mask = 2**bit
    pairs = [(source, source ^ mask) for source in range(lax.axis_size(axis))]
    return lax.ppermute(value, axis, pairs)


def rms_scale(values):
    return values * lax.rsqrt(jnp.mean(values * values, axis=-1, keepdims=True) + EPS)


def pair_gates(logits, chosen_ids):
    experts = jnp.arange(logits.shape[-1])
    picked = jnp.sum(
        jnp.where(chosen_ids[:, :, None] == experts[None, None, :], logits[:, None, :], 0.0),
        axis=-1,
    )
    first = jax.nn.sigmoid(picked[:, 0] - picked[:, 1])
    second = jax.nn.sigmoid(picked[:, 1] - picked[:, 0])
    return jnp.stack([first, second], axis=1)


def merge_parts(first_part, second_part):
    top_first, sum_first, acc_first = first_part
    top_second, sum_second, acc_second = second_part
    highest = jnp.maximum(top_first, top_second)
    scale_first = jnp.exp(top_first - highest)
    scale_second = jnp.exp(top_second - highest)
    merged_sum = sum_first * scale_first + sum_second * scale_second
    merged_acc = acc_first * scale_first[..., None] + acc_second * scale_second[..., None]
    return (highest, merged_sum, merged_acc)


def local(
    residual,
    queries,
    new_entries,
    key_cache,
    value_cache,
    lengths,
    attention_ids,
    expert_ids,
    attention_router,
    expert_router,
    attention_output,
    expert_gain,
    expert_gate,
    expert_up,
    expert_down,
    final_gain,
    unembedding,
    tenant_sizes,
    guidance,
):
    factor_scale = 1.0 / math.sqrt(HD)
    slot_rows = queries.shape[1]
    positions_local = key_cache.shape[2]
    feature_width = H * HD
    blk_index = lax.axis_index("blk")
    linear_index = blk_index * lax.axis_size("req") + lax.axis_index("req")
    query_heads = queries[0].reshape(slot_rows, TOPK, H, HD)
    key_heads = key_cache[0].reshape(slot_rows, positions_local, H, HD)
    value_heads = value_cache[0].reshape(slot_rows, positions_local, H, HD)
    scores = (
        jnp.einsum("rkhd,rphd->rkhp", query_heads, key_heads, preferred_element_type=jnp.float32)
        * factor_scale
    )
    positions = blk_index * positions_local + jnp.arange(positions_local)
    live = (positions[None, :] < lengths[0][:, None])[:, None, None, :]
    local_top = jnp.max(jnp.where(live, scores, -1e30), axis=-1)
    weights_local = jnp.where(live, jnp.exp(scores - local_top[..., None]), 0.0)
    weight_sums = jnp.sum(weights_local, axis=-1)
    weighted = jnp.einsum(
        "rkhp,rphd->rkhd",
        weights_local.astype(jnp.bfloat16),
        value_heads,
        preferred_element_type=jnp.float32,
    )
    highest, weight_sums, weighted = joined((local_top, weight_sums, weighted), "blk", merge_parts)
    new_keys = new_entries[0][:, 0].reshape(slot_rows, H, HD)
    new_values = new_entries[0][:, 1].reshape(slot_rows, H, HD)
    new_score = (
        jnp.einsum("rkhd,rhd->rkh", query_heads, new_keys, preferred_element_type=jnp.float32)
        * factor_scale
    )
    peak = jnp.maximum(highest, new_score)
    shrink = jnp.exp(highest - peak)
    fresh = jnp.exp(new_score - peak)
    denominator = weight_sums * shrink + fresh
    fresh_rounded = fresh.astype(jnp.bfloat16)
    numerator = weighted * shrink[..., None] + jnp.einsum(
        "rkh,rhd->rkhd", fresh_rounded, new_values, preferred_element_type=jnp.float32
    )
    attention_out = (
        (numerator / denominator[..., None])
        .astype(jnp.bfloat16)
        .reshape(slot_rows, TOPK, feature_width)
    )
    inputs = residual[0].astype(jnp.float32)
    normed_input = rms_scale(inputs).astype(jnp.bfloat16)
    attention_gates = pair_gates(
        jnp.dot(normed_input, attention_router, preferred_element_type=jnp.float32), attention_ids
    )
    proj_rows = attention_output.shape[0]
    first_row = linear_index * proj_rows
    own_expert = first_row // feature_width
    own_column = first_row % feature_width
    picked = (attention_ids == own_expert).astype(jnp.float32) * attention_gates
    columns = lax.dynamic_slice_in_dim(
        lax.all_gather(attention_out, "req", axis=0, tiled=True), own_column, proj_rows, 2
    ).astype(jnp.float32)
    selected = jnp.sum(picked[:, :, None] * columns, axis=1).astype(jnp.bfloat16)
    proj_terms = jnp.dot(selected, attention_output, preferred_element_type=jnp.float32)
    attention_proj = lax.psum(proj_terms, ("blk", "req"))
    middle = inputs + attention_proj
    expert_input = (rms_scale(middle) * expert_gain.astype(jnp.float32)).astype(jnp.bfloat16)
    expert_gates = pair_gates(
        jnp.dot(expert_input, expert_router, preferred_element_type=jnp.float32), expert_ids
    )
    hidden_rows = expert_gate.shape[0]
    hidden_expert = linear_index * hidden_rows // FF
    expert_share = jnp.sum((expert_ids == hidden_expert).astype(jnp.float32) * expert_gates, axis=1)
    gate_values = jnp.einsum(
        "rd,fd->rf", expert_input, expert_gate, preferred_element_type=jnp.float32
    )
    up_values = jnp.einsum("rd,fd->rf", expert_input, expert_up, preferred_element_type=jnp.float32)
    expert_hidden = (jax.nn.silu(gate_values) * up_values * expert_share[:, None]).astype(
        jnp.bfloat16
    )
    expert_terms = jnp.dot(expert_hidden, expert_down, preferred_element_type=jnp.float32)
    expert_out = lax.psum(expert_terms, ("blk", "req"))
    final_input = (rms_scale(middle + expert_out) * final_gain.astype(jnp.float32)).astype(
        jnp.bfloat16
    )
    logits = jnp.einsum("rd,vd->rv", final_input, unembedding, preferred_element_type=jnp.float32)
    stream_index = lax.axis_index("cfg")
    half_rows = logits.shape[0] // 2
    own_rows = lax.dynamic_slice_in_dim(logits, stream_index * half_rows, half_rows, 0)
    other_rows = lax.dynamic_slice_in_dim(logits, (1 - stream_index) * half_rows, half_rows, 0)
    partner = swapped(other_rows, "cfg", 0)
    first_stream = stream_index == 0
    conditional = jnp.where(first_stream, own_rows, partner)
    unconditional = jnp.where(first_stream, partner, own_rows)
    request_index = stream_index * half_rows + jnp.arange(half_rows)
    tenant_ends = jnp.cumsum(tenant_sizes)
    tenant = jnp.sum((request_index[:, None] >= tenant_ends[None, :]).astype(jnp.int32), axis=1)
    tenant_onehot = tenant[:, None] == jnp.arange(tenant_sizes.shape[0])[None, :]
    factor = (
        jnp.sum(jnp.where(tenant_onehot, guidance[None, :], 0), axis=1).astype(jnp.float32) / 4.0
    )
    return unconditional + factor[:, None] * (conditional - unconditional)


def solution(mesh):
    placed = (
        P("cfg", None, None),
        P("cfg", "req", None),
        P("cfg", "req", None, None),
        P("cfg", "req", "blk", None),
        P("cfg", "req", "blk", None),
        P("cfg", "req"),
        P(),
        P(),
        P(),
        P(),
        P(("blk", "req"), None),
        P(),
        P(("blk", "req"), None),
        P(("blk", "req"), None),
        P(("blk", "req"), None),
        P(),
        P(("blk", "req"), None),
        P(),
        P(),
    )
    return jax.shard_map(
        local, mesh=mesh, in_specs=placed, out_specs=P("cfg", ("blk", "req")), check_vma=False
    )
```

profile of v0, /device:TPU:1, one launch (start us, length us, event | category | flops | bytes accessed | tf_op | source)
XLA Modules:
  0.0 1075.7 jit_solution(13136947409741794824)
XLA Ops:
  6.6 0.9 copy.72
  7.4 1.3 copy.71
  12.1 83.0 %all-gather.1 = bf16[256,2,16]{2,1,0:T(2,128)(2,1)S(1)} all-gather(bf16[4,2,16]{2,1,0:T(2,128)(2,1)S(1)} %copy.66), channel_id=3, replica_groups=mesh['cfg'=2,'blk'=64,'req'=4] {'blk'}, dimensions={0}, use_global_device_ids=true | all-gather | bytes 16640 | tf_op jit(solution)/shard_map/all_gather | solution.py:19
  95.2 76.2 %all-gather = bf16[256,2,16]{2,1,0:T(2,128)(2,1)S(1)} all-gather(bf16[4,2,16]{2,1,0:T(2,128)(2,1)S(1)} %copy.64), channel_id=2, replica_groups=mesh['cfg'=2,'blk'=64,'req'=4] {'blk'}, dimensions={0}, use_global_device_ids=true | all-gather | bytes 16640 | tf_op jit(solution)/shard_map/all_gather | solution.py:19
  172.3 58.7 %while.19 = (s32[]{:T(128)}, f32[4,2,16]{2,1,0:T(2,128)S(1)}, f32[4,2,16]{2,1,0:T(2,128)S(1)}, f32[4,2,16,128]{3,2,1,0:T(8,128)S(1)}, bf16[64,4,2,16]{3,2,1,0:T(...) while((s32[]{:T(128)}, f32[4,2,16]{2,1,0:T(2,128)S(1)}, ...), condition=%wide.region_5.6_spmd, body=%wide.region_4.5_spmd.sunk | while | flops 66565 | bytes 168599 | solution.py:27
  176.1 0.9 fusion.61
  177.9 0.9 fusion.61
  182.6 0.9 fusion.61
  189.1 0.9 fusion.61
  193.8 0.9 fusion.61
  195.6 0.9 fusion.61
  200.3 0.9 fusion.61
  206.8 0.9 fusion.61
  211.5 0.9 fusion.61
  213.4 0.9 fusion.61
  231.2 9.6 all_gather.21
  242.1 420.9 %all-reduce.3.cloned.1.call-done = f32[16,2048]{1,0:T(8,128)} async-done(((f32[16,2048]{1,0:T(8,128)}), f32[16,2048]{1,0:T(8,128)}) %all-reduce.3.cloned.1.call-update) | async-done | bytes 131088 | tf_op jit(solution)/shard_map/psum | solution.py:144
  663.0 1.1 multiply_reduce_fusion.1
  664.1 1.0 multiply_convert_fusion.1
  665.7 1.3 fusion.7
  667.2 385.1 %all-reduce.5.cloned.1.call-done = f32[16,2048]{1,0:T(8,128)} async-done(((f32[16,2048]{1,0:T(8,128)}), f32[16,2048]{1,0:T(8,128)}) %all-reduce.5.cloned.1.call-update) | async-done | bytes 131088 | tf_op jit(solution)/shard_map/psum | solution.py:161
  1052.4 1.0 multiply_reduce_fusion
  1053.5 1.2 fusion.12
  1054.6 13.0 %collective-permute-start = (f32[8,125]{1,0:T(8,128)S(1)}, f32[8,125]{1,0:T(8,128)S(1)}, u32[]{:S(2)}, u32[]{:S(2)}) collective-permute-start(f32[8,125]{1,0:T(8,128)S(1)} %constant_dynamic-slice_fusion), channel_id=1, source_target_pairs={{0,256},{256,0},{1,257},{257,1},{2,258},{258,2},{3,259},{259,3},{4... | collective-permute-start | bytes 12008 | tf_op jit(solution)/shard_map/ppermute | solution.py:35
  (204 shorter events, 55.9 us)
Async XLA Ops:
  6.5 659.1 %copy-start = (bf16[176,2048]{1,0:T(8,128)(2,1)S(1)}, bf16[176,2048]{1,0:T(8,128)(2,1)}, u32[]{:S(2)}) copy-start(bf16[176,2048]{1,0:T(8,128)(2,1)} %param.35) | copy-start | bytes 2162692
  6.5 2.2 copy-start.3
  6.5 2.4 copy-start.15
  6.5 165.0 %all-gather.5.cloned.1.call-start = ((), (), s32[]{:S(2)}) async-start(), calls=%async_computation.2 | async-start | bytes 2129920 | tf_op jit(solution)/shard_map/all_gather | solution.py:19
  8.7 2.6 copy-start.9
  8.9 2.7 copy-start.2
  8.9 2.8 copy-start.14
  8.9 3.0 copy-start.12
  9.6 231.4 %copy-start.7 = (bf16[64,2048]{1,0:T(8,128)(2,1)S(1)}, bf16[64,2048]{1,0:T(8,128)(2,1)}, u32[]{:S(2)}) copy-start(bf16[64,2048]{1,0:T(8,128)(2,1)} %param.31) | copy-start | bytes 786436
  10.0 231.9 %copy-start.10 = (bf16[2048]{0:T(1024)(128)(2,1)S(1)}, bf16[2048]{0:T(1024)(128)(2,1)}, u32[]{:S(2)}) copy-start(bf16[2048]{0:T(1024)(128)(2,1)} %param.32) | copy-start | bytes 12292
  10.0 231.9 %copy-start.16 = (s32[4]{0:T(128)S(1)}, s32[4]{0:T(128)}, u32[]{:S(2)}) copy-start(s32[4]{0:T(128)} %param.38) | copy-start | bytes 52
  10.1 655.1 %copy-start.8 = (bf16[2048,8]{0,1:T(8,128)(2,1)S(1)}, bf16[2048,8]{0,1:T(8,128)(2,1)}, u32[]{:S(2)}) copy-start(bf16[2048,8]{0,1:T(8,128)(2,1)} %param.30) | copy-start | bytes 98308
  10.1 655.2 %copy-start.13 = (s32[16,2]{0,1:T(2,128)S(1)}, s32[16,2]{0,1:T(2,128)}, u32[]{:S(2)}) copy-start(s32[16,2]{0,1:T(2,128)} %param.28) | copy-start | bytes 388
  10.1 655.3 %copy-start.4 = (bf16[176,2048]{1,0:T(8,128)(2,1)S(1)}, bf16[176,2048]{1,0:T(8,128)(2,1)}, u32[]{:S(2)}) copy-start(bf16[176,2048]{1,0:T(8,128)(2,1)} %param.33) | copy-start | bytes 2162692
  10.7 652.3 %all-reduce.3.cloned.1.call-start = ((), (), s32[]{:S(2)}) async-start(), calls=%async_computation | async-start | bytes 262144 | tf_op jit(solution)/shard_map/psum | solution.py:144
  12.0 653.7 %copy-start.5 = (bf16[176,2048]{1,0:T(8,128)(2,1)S(1)}, bf16[176,2048]{1,0:T(8,128)(2,1)}, u32[]{:S(2)}) copy-start(bf16[176,2048]{1,0:T(8,128)(2,1)} %param.34) | copy-start | bytes 2162692
  231.0 436.1 %copy-start.11 = (bf16[2048]{0:T(1024)(128)(2,1)S(1)}, bf16[2048]{0:T(1024)(128)(2,1)}, u32[]{:S(2)}) copy-start(bf16[2048]{0:T(1024)(128)(2,1)} %param.36) | copy-start | bytes 12292
  231.1 436.1 %copy-start.17 = (s32[4]{0:T(128)S(1)}, s32[4]{0:T(128)}, u32[]{:S(2)}) copy-start(s32[4]{0:T(128)} %param.39) | copy-start | bytes 52
  240.9 812.6 %copy-start.6 = (bf16[125,2048]{1,0:T(8,128)(2,1)S(1)}, bf16[125,2048]{1,0:T(8,128)(2,1)}, u32[]{:S(2)}) copy-start(bf16[125,2048]{1,0:T(8,128)(2,1)} %param.37) | copy-start | bytes 1536004
  241.8 810.6 %all-reduce.5.cloned.1.call-start = ((), (), s32[]{:S(2)}) async-start(), calls=%async_computation.1 | async-start | bytes 262144 | tf_op jit(solution)/shard_map/psum | solution.py:161
  663.0 389.4 %copy-start.1 = (f32[16,2048]{1,0:T(8,128)S(1)}, f32[16,2048]{1,0:T(8,128)}, u32[]{:S(2)}) copy-start(f32[16,2048]{1,0:T(8,128)} %all-reduce.3.cloned.1.call-done) | copy-start | bytes 393220
  1054.6 13.8 %collective-permute-start = (f32[8,125]{1,0:T(8,128)S(1)}, f32[8,125]{1,0:T(8,128)S(1)}, u32[]{:S(2)}, u32[]{:S(2)}) collective-permute-start(f32[8,125]{1,0:T(8,128)S(1)} %constant_dynamic-slice_fusion), channel_id=1, source_target_pairs={{0,256},{256,0},{1,257},{257,1},{2,258},{258,2},{3,259},{259,3},{4... | collective-permute-start | bytes 12008 | tf_op jit(solution)/shard_map/ppermute | solution.py:35
Sparse Core Ops, SparseCore 0:
  10.8 137.8 all-gather.4
  242.0 421.0 all-reduce.2
  669.3 383.0 all-reduce.4
where the time goes:
time: 1080 us
  waiting for transfers between devices  807 us (75%)
  blocking collectives  169 us (16%)
  other arithmetic  62.9 us (6%)
  between operations  13.5 us (1%)
  starting transfers between devices  13.1 us (1%)
    psum x1, waiting for transfers between devices, local(): attention_proj = lax.psum(proj_terms, ('blk', 'req'))  421 us
    psum x1, waiting for transfers between devices, local(): expert_out = lax.psum(expert_terms, ('blk', 'req'))  385 us
    all_gather x2, blocking collectives, joined(): lax.all_gather(part.astype(kind), axis)  159 us
    add x63, other arithmetic, merge_parts(): acc_first * scale_first[..., None] + acc_second * scale_second[..., None]  55 us
  transfers between devices with their start and end apart: 4, of which 3 were waited for; matrix products, arithmetic and copies ran while one was open for 0% of the time, Pallas kernels for 0%

commit v1 on v0

v1 whole, which is shorter than its diff:
```python
import math

import jax
import jax.numpy as jnp
from jax import lax
from jax.experimental import pallas as pl
from jax.experimental.pallas import tpu as pltpu
from jax.sharding import Mesh
from jax.sharding import PartitionSpec as P

D = 2048
H = 16
HD = 128
FF = 5632
TOPK = 2
EPS = 1e-05
NEG = -1e30
LANES = 128
HEADS_ROW = 4
ROW = HEADS_ROW * HD + LANES
SCALE = 1.0 / math.sqrt(HD)

F32 = jnp.float32
BF16 = jnp.bfloat16
NT = (((1,), (1,)), ((), ()))


def vmem():
    return pl.BlockSpec(memory_space=pltpu.VMEM)


def smem():
    return pl.BlockSpec(memory_space=pltpu.SMEM)


def call(body, outs, specs, scratch=()):
    return pl.pallas_call(
        body,
        out_shape=outs,
        in_specs=specs,
        out_specs=jax.tree.map(lambda _: vmem(), outs),
        scratch_shapes=list(scratch),
        compiler_params=pltpu.CompilerParams(vmem_limit_bytes=48 * 1024 * 1024),
    )


def iota(shape, dim):
    return lax.broadcasted_iota(jnp.int32, shape, dim)


def dot(a, b):
    return jnp.dot(a, b, preferred_element_type=F32)


def rms(values):
    return lax.rsqrt(jnp.mean(values * values, axis=-1, keepdims=True) + EPS)


def expert_of_plane():
    return lax.axis_index("z") // 2


def share_column(logits_t, ids_ref, expert, lane_of_row):
    experts = iota(logits_t.shape, 0)
    first_id, second_id = ids_ref[0:1, :], ids_ref[1:2, :]
    first = jnp.sum(jnp.where(experts == first_id, logits_t, 0.0), axis=0, keepdims=True)
    second = jnp.sum(jnp.where(experts == second_id, logits_t, 0.0), axis=0, keepdims=True)
    gate_first = 1.0 / (1.0 + jnp.exp(second - first))
    gate_second = 1.0 / (1.0 + jnp.exp(first - second))
    share = jnp.where(first_id == expert, gate_first, 0.0) + jnp.where(
        second_id == expert, gate_second, 0.0
    )
    lanes = iota((lane_of_row.shape[0], share.shape[1]), 1)
    return jnp.sum(jnp.where(lanes == lane_of_row, share, 0.0), axis=1, keepdims=True)


def attend_kernel(
    q_ref, k_ref, v_ref, new_ref, lengths_ref, ids_ref, out_ref, rows_ref
):
    requests, positions = k_ref.shape[1], k_ref.shape[2]
    block = lax.axis_index("z") * lax.axis_size("x") + lax.axis_index("x")
    first_request = lax.axis_index("req") * requests
    queries = q_ref[0].astype(F32)
    own_head = iota((H, D), 0) == iota((H, D), 1) // HD
    place = block * positions + iota((1, positions), 1)
    sub = iota((8, LANES), 0)
    lane = iota((8, LANES), 1)
    for r in range(requests):
        wide = jnp.concatenate(
            [
                jnp.where(own_head, queries[r : r + 1, k * D : (k + 1) * D], 0.0)
                for k in range(TOPK)
            ],
            axis=0,
        )
        scores = (
            lax.dot_general(wide.astype(BF16), k_ref[0, r], NT, preferred_element_type=F32) * SCALE
        )
        entry = new_ref[0, r].astype(F32)
        new_score = jnp.sum(wide * entry[0:1, :], axis=1, keepdims=True) * SCALE
        live = place < lengths_ref[0, r]
        owner = block == 0
        top = jnp.max(jnp.where(live, scores, NEG), axis=1, keepdims=True)
        top = jnp.maximum(top, jnp.where(owner, new_score, NEG))
        peak = top.astype(BF16).astype(F32)
        weights = jnp.where(live, jnp.exp(scores - peak), 0.0)
        fresh = jnp.where(owner, jnp.exp(new_score - peak), 0.0)
        total = jnp.sum(weights, axis=1, keepdims=True) + fresh
        high = total.astype(BF16).astype(F32)
        low = total - high
        values = dot(weights.astype(BF16), v_ref[0, r])
        values = values + fresh.astype(BF16).astype(F32) * entry[1:2, :]
        for k in range(TOPK):
            for quarter in range(H // HEADS_ROW):
                half, group = quarter // 2, quarter % 2
                base = k * H + (quarter // 2) * 8
                parts = []
                for j in range(HEADS_ROW):
                    head = quarter * HEADS_ROW + j
                    tile = values[base : base + 8, head * HD : (head + 1) * HD]
                    parts.append(jnp.sum(jnp.where(sub == head % 8, tile, 0.0), axis=0, keepdims=True))
                column = sub - group * HEADS_ROW
                here = (column >= 0) & (column < HEADS_ROW)
                stats = jnp.where(lane == column, peak[base : base + 8], 0.0)
                stats = stats + jnp.where(lane == column + 4, high[base : base + 8], 0.0)
                stats = stats + jnp.where(lane == column + 8, low[base : base + 8], 0.0)
                parts.append(jnp.sum(jnp.where(here, stats, 0.0), axis=0, keepdims=True))
                row = group * requests + r
                rows_ref[half, k, row : row + 1, :] = jnp.concatenate(parts, axis=1)
    request = iota((8, 1), 0) % requests
    chosen = []
    for k in range(TOPK):
        picked = jnp.zeros((8, 1), jnp.int32)
        for r in range(requests):
            picked = jnp.where(request == r, ids_ref[first_request + r, k], picked)
        chosen.append(picked)
    for plane in range(out_ref.shape[0]):
        expert, half = plane // 2, plane % 2
        message = jnp.where(chosen[0] == expert, rows_ref[half, 0], 0.0)
        message = message + jnp.where(chosen[1] == expert, rows_ref[half, 1], 0.0)
        out_ref[plane] = message.astype(BF16)


def spread_lanes(first_lane):
    rows, columns = iota((LANES, HEADS_ROW * HD), 0), iota((LANES, HEADS_ROW * HD), 1)
    return rows == first_lane + columns // HD


def merged(parts, stats, groups):
    count = stats.shape[0]
    peak = jnp.max(stats, axis=0)
    scale = jnp.exp(stats - peak[None])
    rows = count * groups * 8
    flat = scale.reshape(rows, LANES)
    high = flat.astype(BF16)
    low = (flat - high.astype(F32)).astype(BF16)
    lift = spread_lanes(0).astype(BF16)
    scales = dot(high, lift) + dot(low, lift)
    sums = dot(
        stats.reshape(rows, LANES).astype(BF16), (spread_lanes(4) | spread_lanes(8)).astype(BF16)
    )
    numerator, denominator = [], []
    for g in range(groups):
        top, bottom = 0.0, 0.0
        for n in range(count):
            at = (n * groups + g) * 8
            factor = scales[at : at + 8]
            top = top + parts(n, g) * factor
            bottom = bottom + sums[at : at + 8] * factor
        numerator.append(top)
        denominator.append(bottom)
    return numerator, denominator, peak


def merge_kernel(in_ref, weight_ref, out_ref):
    wide = HEADS_ROW * HD
    copies = out_ref.shape[0]
    stats = in_ref[:, :, wide:].astype(F32)[:, None]
    numerator, denominator, peak = merged(
        lambda n, g: in_ref[n, :, :wide].astype(F32), stats, 1
    )
    lane = iota((8, LANES), 1)
    packed = jnp.where(lane < HEADS_ROW, peak[0], 0.0)
    for j in range(HEADS_ROW):
        total = denominator[0][:, j * HD : (j + 1) * HD]
        high = total.astype(BF16).astype(F32)
        packed = jnp.where(lane == 4 + j, high, packed)
        packed = jnp.where(lane == 8 + j, total - high, packed)
    blocks = [numerator[0][:, j * HD : (j + 1) * HD] for j in range(HEADS_ROW)] + [packed]
    blocks = [block.astype(BF16) for block in blocks]
    for copy in range(copies):
        for j, block in enumerate(blocks):
            out_ref[copy, j * 8 : (j + 1) * 8, :] = block
        out_ref[copy, len(blocks) * 8 :, :] = weight_ref[:, copy * LANES : (copy + 1) * LANES]


def project_kernel(in_ref, residual_ref, router_ref, ids_ref, out_ref, stats_ref, weight_ref):
    requests = 4
    columns, groups = 4, 4
    head_rows = HEADS_ROW * 8
    weight_rows = in_ref.shape[1] - head_rows - 8
    sources = in_ref.shape[0]
    expert = expert_of_plane()
    for source in range(sources):
        stats_ref[source] = in_ref[source, head_rows : head_rows + 8, :].astype(F32)
        weight_ref[source * weight_rows : (source + 1) * weight_rows, :] = in_ref[
            source, head_rows + 8 :, :
        ]
    stats = stats_ref[...].reshape(columns, groups, 8, LANES)

    def part(n, g):
        source = n * groups + g
        return jnp.concatenate(
            [in_ref[source, j * 8 : (j + 1) * 8, :] for j in range(HEADS_ROW)], axis=1
        ).astype(F32)

    numerator, denominator, _ = merged(part, stats, groups)
    inputs = residual_ref[0].astype(F32)
    normed = (inputs * rms(inputs)).astype(BF16)
    logits = lax.dot_general(router_ref[...], normed, NT, preferred_element_type=F32)
    row = iota((8 * groups, 1), 0)
    gate = share_column(logits, ids_ref, expert, row // 8 * requests + row % requests)
    attended = jnp.concatenate(
        [top / jnp.maximum(bottom, 1e-30) for top, bottom in zip(numerator, denominator)], axis=0
    )
    gated = (attended.astype(BF16).astype(F32) * gate).astype(BF16)
    wide = HEADS_ROW * HD
    lower = dot(gated, weight_ref[:wide, :])
    upper = dot(gated, weight_ref[wide:, :])
    mixed = jnp.where(row % 8 < requests, lower, upper)
    sub = iota((8, LANES), 0)
    tiles = []
    for g in range(groups):
        tile = mixed[g * 8 : (g + 1) * 8]
        tiles.append(tile + pltpu.roll(tile, 4, 0))
    for pair in range(groups // 2):
        both = jnp.where(sub < requests, tiles[2 * pair], tiles[2 * pair + 1]).astype(BF16)
        for copy in range(out_ref.shape[0]):
            out_ref[copy, pair * 8 : (pair + 1) * 8, :] = both


def fold_kernel(in_ref, out_ref):
    total = in_ref[0].astype(F32)
    for n in range(1, in_ref.shape[0]):
        total = total + in_ref[n].astype(F32)
    total = total.astype(BF16)
    for copy in range(out_ref.shape[0]):
        out_ref[copy] = total


def expert_kernel(
    in_ref, residual_ref, gain_ref, router_ref, ids_ref, gate_ref, up_ref, down_ref, out_ref, middle_ref
):
    chunks = in_ref.shape[0]
    requests = in_ref.shape[1]
    for chunk in range(chunks):
        at = slice(chunk * LANES, (chunk + 1) * LANES)
        middle_ref[:, at] = residual_ref[0, :, at].astype(F32) + in_ref[chunk].astype(F32)
    middle = middle_ref[...]
    inputs = (middle * rms(middle) * gain_ref[...].astype(F32)).astype(BF16)
    logits = lax.dot_general(router_ref[...], inputs, NT, preferred_element_type=F32)
    share = share_column(logits, ids_ref, expert_of_plane(), iota((requests, 1), 0))
    gate = lax.dot_general(inputs, gate_ref[...], NT, preferred_element_type=F32)
    up = lax.dot_general(inputs, up_ref[...], NT, preferred_element_type=F32)
    hidden = (gate / (1.0 + jnp.exp(-gate)) * up * share).astype(BF16)
    for chunk in range(chunks):
        at = slice(chunk * LANES, (chunk + 1) * LANES)
        out_ref[chunk] = dot(hidden, down_ref[:, at]).astype(BF16)


def finish_kernel(in_ref, attention_ref, residual_ref, out_ref):
    total = attention_ref[0].astype(F32)
    for n in range(1, attention_ref.shape[0]):
        total = total + attention_ref[n].astype(F32)
    for n in range(in_ref.shape[0]):
        total = total + in_ref[n].astype(F32)
    chunk = lax.axis_index("x") * lax.axis_size("req") + lax.axis_index("req")
    at = pl.ds(pl.multiple_of(chunk * LANES, LANES), LANES)
    total = (total + residual_ref[0, :, at].astype(F32)).astype(out_ref.dtype)
    half = out_ref.shape[1]
    copies = out_ref.shape[0] // 2
    for stream in range(2):
        for copy in range(copies):
            out_ref[stream * copies + copy] = total[stream * half : (stream + 1) * half]


def head_kernel(in_ref, gain_ref, words_ref, sizes_ref, guidance_ref, out_ref, joined_ref):
    half = in_ref.shape[1]
    chunks = in_ref.shape[0] // 2
    for stream in range(2):
        for chunk in range(chunks):
            at = slice(chunk * LANES, (chunk + 1) * LANES)
            joined_ref[stream * half : (stream + 1) * half, at] = in_ref[
                stream * chunks + chunk
            ].astype(F32)
    joined = joined_ref[...]
    inputs = (joined * rms(joined) * gain_ref[...].astype(F32)).astype(BF16)
    logits = lax.dot_general(inputs, words_ref[...], NT, preferred_element_type=F32)
    request = lax.axis_index("cfg") * half + iota((half, 1), 0)
    tenants = sizes_ref.shape[0]
    tenant = jnp.zeros((half, 1), jnp.int32)
    end = 0
    for t in range(tenants):
        end = end + sizes_ref[t]
        tenant = tenant + (request >= end).astype(jnp.int32)
    chosen = jnp.zeros((half, 1), jnp.int32)
    for t in range(tenants):
        chosen = jnp.where(tenant == t, guidance_ref[t], chosen)
    factor = chosen.astype(F32) / 4.0
    conditional, unconditional = logits[:half], logits[half:]
    out_ref[...] = unconditional + factor * (conditional - unconditional)


def exchanged(value, axis):
    return lax.all_to_all(value, axis, 0, 0, tiled=True)


def local(
    residual,
    queries,
    new_entries,
    key_cache,
    value_cache,
    lengths,
    attention_ids,
    expert_ids,
    attention_router,
    expert_router,
    attention_output,
    expert_gain,
    expert_gate,
    expert_up,
    expert_down,
    final_gain,
    unembedding,
    tenant_sizes,
    guidance,
):
    planes = lax.axis_size("z")
    plane = ("x", "req")
    members = lax.axis_size(plane)
    requests = residual.shape[1]
    shape = jax.ShapeDtypeStruct

    partial = call(
        attend_kernel,
        shape((planes, 8, ROW), BF16),
        [vmem()] * 4 + [smem()] * 2,
        [pltpu.VMEM((2, TOPK, 8, ROW), F32)],
    )(queries, key_cache, value_cache, new_entries, lengths, attention_ids)
    partial = exchanged(partial, "z")

    weight_rows = attention_output.shape[0]
    merged_rows = HEADS_ROW * 8 + 8 + weight_rows
    both = call(merge_kernel, shape((members, merged_rows, LANES), BF16), [vmem()] * 2)(
        partial, attention_output
    )
    both = exchanged(both, plane)

    chunk = shape((planes, requests, LANES), BF16)
    projected = call(
        project_kernel,
        chunk,
        [vmem()] * 4,
        [pltpu.VMEM((members, 8, LANES), F32), pltpu.VMEM((members * weight_rows, LANES), BF16)],
    )(both, residual, attention_router.T, attention_ids.T)
    projected = exchanged(projected, "z")

    spread = shape((members, requests, LANES), BF16)
    attention = call(fold_kernel, spread, [vmem()])(projected)
    attention = exchanged(attention, plane)

    hidden = call(
        expert_kernel, spread, [vmem()] * 8, [pltpu.VMEM((requests, D), F32)]
    )(
        attention,
        residual,
        expert_gain[None],
        expert_router.T,
        expert_ids.T,
        expert_gate,
        expert_up,
        expert_down,
    )
    hidden = exchanged(hidden, plane)
    hidden = call(fold_kernel, chunk, [vmem()])(hidden)
    hidden = exchanged(hidden, "z")

    streams = lax.axis_size("cfg")
    final = call(
        finish_kernel, shape((streams * members, requests // 2, LANES), BF16), [vmem()] * 3
    )(hidden, projected, residual)
    final = exchanged(final, ("cfg",) + plane)

    return call(
        head_kernel,
        shape((requests // 2, unembedding.shape[0]), F32),
        [vmem()] * 3 + [smem()] * 2,
        [pltpu.VMEM((requests, D), F32)],
    )(final, final_gain[None], unembedding, tenant_sizes, guidance)


def solution(mesh):
    sizes = mesh.devices.shape
    split = Mesh(mesh.devices.reshape(sizes[0], 16, sizes[1] // 16, sizes[2]), ("cfg", "z", "x", "req"))
    blk = ("z", "x")
    rows = P(("z", "x", "req"), None)
    placed = (
        P("cfg", None, None),
        P("cfg", "req", None),
        P("cfg", "req", None, None),
        P("cfg", "req", blk, None),
        P("cfg", "req", blk, None),
        P("cfg", "req"),
        P(),
        P(),
        P(),
        P(),
        rows,
        P(),
        rows,
        rows,
        rows,
        P(),
        rows,
        P(),
        P(),
    )
    return jax.shard_map(
        local,
        mesh=split,
        in_specs=placed,
        out_specs=P("cfg", ("z", "x", "req")),
        check_vma=False,
    )
```

time: 1080 us -> 128 us (0.12)
  waiting for transfers between devices: 807 us -> 13.6 us
  blocking collectives: 169 us -> 86.1 us
  other arithmetic: 62.9 us -> 0 us
  between operations: 13.5 us -> 0.16 us
    psum x2 -> x0, waiting for transfers between devices: 806 us -> none  [the longest x1 421 us: local(): attention_proj = lax.psum(proj_terms, ('blk', 'req'))]
    all_gather x3 -> x0, blocking collectives: 169 us -> none  [the longest x2 159 us: joined(): lax.all_gather(part.astype(kind), axis)]
    all_to_all x0 -> x5, blocking collectives: none -> 86.1 us  [exchanged(): return lax.all_to_all(value, axis, 0, 0, tiled=True)]
    add x130 -> x0, other arithmetic: 57.7 us -> none  [the longest x63 55 us: merge_parts(): acc_first * scale_first[..., None] + acc_second * scale_second[..., None]]
    all_to_all x0 -> x2, starting transfers between devices: none -> 15.5 us  [exchanged(): return lax.all_to_all(value, axis, 0, 0, tiled=True)]
    all_to_all x0 -> x2, waiting for transfers between devices: none -> 13.6 us  [exchanged(): return lax.all_to_all(value, axis, 0, 0, tiled=True)]
    ppermute x1 -> x0, starting transfers between devices: 13 us -> none  [swapped(): return lax.ppermute(value, axis, pairs)]
  transfers between devices with their start and end apart: 4 -> 2, of which waited for: 3 -> 2; matrix products, arithmetic and copies ran while one was open for 0% -> 0% of each run, Pallas kernels for 0% -> 0%
where the time goes in v1:
time: 128 us; the launch traced here: 127 us
  blocking collectives  86.1 us (67%)
  starting transfers between devices  15.5 us (12%)
  waiting for transfers between devices  13.6 us (11%)
  Pallas kernels  6.71 us (5%)
  local copies, waits for them, and re-layouts  5.29 us (4%)
    all_to_all x5, blocking collectives, exchanged(): return lax.all_to_all(value, axis, 0, 0, tiled=True)  86.1 us
    all_to_all x2, starting transfers between devices, exchanged(): return lax.all_to_all(value, axis, 0, 0, tiled=True)  15.5 us
    all_to_all x2, waiting for transfers between devices, exchanged(): return lax.all_to_all(value, axis, 0, 0, tiled=True)  13.6 us
    unnamed x39, local copies, waits for them, and re-layouts  5.27 us
  transfers between devices with their start and end apart: 2, of which 2 were waited for; matrix products, arithmetic and copies ran while one was open for 0% of the time, Pallas kernels for 0%

profile of v1, /device:TPU:1, one launch (start us, length us, event | category | flops | bytes accessed | tf_op | source)
XLA Modules:
  0.0 127.3 jit_solution(10770594736178713722)
XLA Ops:
  0.0 0.8 copy.20.ids_ref
  0.8 1.1 copy-done
  1.9 1.1 copy-done.1
  3.0 0.8 copy-done.8
  3.8 0.8 copy-done.9
  4.6 2.1 %shard_map.181 = bf16[16,8,640]{2,1,0:T(8,128)(2,1)S(1)} custom-call(bf16[1,4,4096]{2,1,0:T(4,128)(2,1)S(1)} %copy-done.8, bf16[1,4,48,2048]{3,2,1,0:T(8,128)(2,1)S(1)} %copy-done, bf16[1,4,48,2048]{3,2,1,0:T(8,128)(2,1)S(1)} %copy-done.1, bf16[1,4,2,2048]{3,2,1,0:T(2,128)(2,1)S(1)} %copy-done.9, s32[1,4]{1,0:T(1,128)S(1)} %copy-done.16, ...), custom_call_target="tpu_custom_call" | custom-call | tf_op jit(solution)/shard_map/pallas_call | solution.py:345
  6.7 0.0 copy-start.7
  6.7 27.9 %all_to_all.35.in_ref = bf16[16,8,640]{2,1,0:T(8,128)(2,1)S(1)} all-to-all(bf16[16,8,640]{2,1,0:T(8,128)(2,1)S(1)} %shard_map.181), channel_id=1, replica_groups=mesh['cfg'=2,'z'=16,'x'=4,'req'=4] {'z'}, dimensions={0} | all-to-all | bytes 327680 | tf_op jit(solution)/shard_map/all_to_all | solution.py:315
  34.6 0.3 shard_map.182
  34.9 0.0 copy-start.2
  34.9 14.8 %all_to_all.36.in_ref = bf16[16,104,128]{2,1,0:T(8,128)(2,1)S(1)} all-to-all(bf16[16,104,128]{2,1,0:T(8,128)(2,1)S(1)} %shard_map.182), channel_id=1, replica_groups=mesh['cfg'=2,'z'=16,'x'=4,'req'=4] {'x','req'}, dimensions={0} | all-to-all | bytes 851968 | tf_op jit(solution)/shard_map/all_to_all | solution.py:315
  49.7 0.6 shard_map.183
  50.3 19.4 %all_to_all.37.in_ref.attention_ref = bf16[16,16,128]{2,1,0:T(8,128)(2,1)S(1)} all-to-all(bf16[16,16,128]{2,1,0:T(8,128)(2,1)S(1)} %shard_map.183), channel_id=1, replica_groups=mesh['cfg'=2,'z'=16,'x'=4,'req'=4] {'z'}, dimensions={0} | all-to-all | bytes 131072 | tf_op jit(solution)/shard_map/all_to_all | solution.py:315
  69.7 0.6 shard_map.184
  70.4 4.4 %all-to-all-start.3 = ((bf16[16,16,128]{2,1,0:T(8,128)(2,1)}), bf16[16,16,128]{2,1,0:T(8,128)(2,1)S(1)}, u32[]{:S(2)}, u32[]{:S(2)}) async-start(bf16[16,16,128]{2,1,0:T(8,128)(2,1)} %shard_map.184), calls=%async_computation.3 | async-start | bytes 131072 | tf_op jit(solution)/shard_map/all_to_all | solution.py:315
  74.8 6.5 %all-to-all-done.3.in_ref = bf16[16,16,128]{2,1,0:T(8,128)(2,1)S(1)} async-done(((bf16[16,16,128]{2,1,0:T(8,128)(2,1)}), bf16[16,16,128]{2,1,0:T(8,128)(2,1)S(1)}, u32[]{:S(2)}, u32[]{:S(2)}) %all-to-all-start.3) | async-done | bytes 65568 | tf_op jit(solution)/shard_map/all_to_all | solution.py:315
  81.3 0.7 copy-done.13
  82.0 0.9 shard_map.185
  82.9 9.6 %all_to_all.38.in_ref = bf16[16,16,128]{2,1,0:T(8,128)(2,1)S(1)} all-to-all(bf16[16,16,128]{2,1,0:T(8,128)(2,1)S(1)} %shard_map.185), channel_id=1, replica_groups=mesh['cfg'=2,'z'=16,'x'=4,'req'=4] {'x','req'}, dimensions={0} | all-to-all | bytes 131072 | tf_op jit(solution)/shard_map/all_to_all | solution.py:315
  92.6 14.4 %all_to_all.39.in_ref = bf16[16,16,128]{2,1,0:T(8,128)(2,1)S(1)} all-to-all(bf16[16,16,128]{2,1,0:T(8,128)(2,1)S(1)} %shard_map.186), channel_id=1, replica_groups=mesh['cfg'=2,'z'=16,'x'=4,'req'=4] {'z'}, dimensions={0} | all-to-all | bytes 131072 | tf_op jit(solution)/shard_map/all_to_all | solution.py:315
  107.0 0.7 shard_map.187
  107.7 11.1 %all-to-all-start.6 = ((bf16[32,8,128]{2,1,0:T(8,128)(2,1)}), bf16[32,8,128]{2,1,0:T(8,128)(2,1)S(1)}, u32[]{:S(2)}, u32[]{:S(2)}) async-start(bf16[32,8,128]{2,1,0:T(8,128)(2,1)} %shard_map.187), calls=%async_computation.6 | async-start | bytes 131072 | tf_op jit(solution)/shard_map/all_to_all | solution.py:315
  118.8 7.1 %all-to-all-done.6.in_ref = bf16[32,8,128]{2,1,0:T(8,128)(2,1)S(1)} async-done(((bf16[32,8,128]{2,1,0:T(8,128)(2,1)}), bf16[32,8,128]{2,1,0:T(8,128)(2,1)S(1)}, u32[]{:S(2)}, u32[]{:S(2)}) %all-to-all-start.6) | async-done | bytes 65568 | tf_op jit(solution)/shard_map/all_to_all | solution.py:315
  125.9 1.5 %shard_map.188 = f32[8,125]{1,0:T(8,128)} custom-call(bf16[32,8,128]{2,1,0:T(8,128)(2,1)S(1)} %all-to-all-done.6.in_ref, bf16[1,2048]{1,0:T(2,128)(2,1)S(1)} %broadcast_in_dim.7.gain_ref, bf16[125,2048]{1,0:T(8,128)(2,1)S(1)} %copy-done.6, s32[4]{0:T(128)S(1)} %copy-done.14, s32[4]{0:T(128)S(1)} %copy-done.15), custom_call_target="tpu_custom_call" | custom-call | tf_op jit(solution)/shard_map/pallas_call | solution.py:395
  (34 shorter events, 0.1 us)
Async XLA Ops:
  0.0 0.8 copy-start.16
  0.8 1.1 copy-start
  1.9 1.1 copy-start.1
  3.0 0.8 copy-start.8
  3.8 0.8 copy-start.9
  6.7 27.9 %copy-start.7 = (bf16[64,2048]{1,0:T(8,128)(2,1)S(1)}, bf16[64,2048]{1,0:T(8,128)(2,1)}, u32[]{:S(2)}) copy-start(bf16[64,2048]{1,0:T(8,128)(2,1)} %weight_ref.1) | copy-start | bytes 786436
  34.6 15.2 %copy-start.5 = (bf16[1,16,2048]{2,1,0:T(8,128)(2,1)S(1)}, bf16[1,16,2048]{2,1,0:T(8,128)(2,1)}, u32[]{:S(2)}) copy-start(bf16[1,16,2048]{2,1,0:T(8,128)(2,1)} %residual_ref.5) | copy-start | bytes 196612
  34.6 15.2 %copy-start.11 = (bf16[2048,8]{0,1:T(8,128)(2,1)S(1)}, bf16[2048,8]{0,1:T(8,128)(2,1)}, u32[]{:S(2)}) copy-start(bf16[2048,8]{0,1:T(8,128)(2,1)} %param.27) | copy-start | bytes 98308
  34.6 15.2 %copy-start.12 = (s32[16,2]{0,1:T(2,128)S(1)}, s32[16,2]{0,1:T(2,128)}, u32[]{:S(2)}) copy-start(s32[16,2]{0,1:T(2,128)} %param.25) | copy-start | bytes 388
  34.6 46.7 %copy-start.4 = (bf16[176,2048]{1,0:T(8,128)(2,1)S(1)}, bf16[176,2048]{1,0:T(8,128)(2,1)}, u32[]{:S(2)}) copy-start(bf16[176,2048]{1,0:T(8,128)(2,1)} %down_ref.1) | copy-start | bytes 2162692
  34.9 46.4 %copy-start.2 = (bf16[176,2048]{1,0:T(8,128)(2,1)S(1)}, bf16[176,2048]{1,0:T(8,128)(2,1)}, u32[]{:S(2)}) copy-start(bf16[176,2048]{1,0:T(8,128)(2,1)} %gate_ref.1) | copy-start | bytes 2162692
  34.9 46.4 %copy-start.3 = (bf16[176,2048]{1,0:T(8,128)(2,1)S(1)}, bf16[176,2048]{1,0:T(8,128)(2,1)}, u32[]{:S(2)}) copy-start(bf16[176,2048]{1,0:T(8,128)(2,1)} %up_ref.1) | copy-start | bytes 2162692
  70.4 4.4 %copy-start.17 = (bf16[2048]{0:T(1024)(128)(2,1)S(1)}, bf16[2048]{0:T(1024)(128)(2,1)}, u32[]{:S(2)}) copy-start(bf16[2048]{0:T(1024)(128)(2,1)} %param.30) | copy-start | bytes 12292
  70.4 11.0 %copy-start.10 = (bf16[2048,8]{0,1:T(8,128)(2,1)S(1)}, bf16[2048,8]{0,1:T(8,128)(2,1)}, u32[]{:S(2)}) copy-start(bf16[2048,8]{0,1:T(8,128)(2,1)} %param.28) | copy-start | bytes 98308
  70.4 10.9 %all-to-all-start.3 = ((bf16[16,16,128]{2,1,0:T(8,128)(2,1)}), bf16[16,16,128]{2,1,0:T(8,128)(2,1)S(1)}, u32[]{:S(2)}, u32[]{:S(2)}) async-start(bf16[16,16,128]{2,1,0:T(8,128)(2,1)} %shard_map.184), calls=%async_computation.3 | async-start | bytes 131072 | tf_op jit(solution)/shard_map/all_to_all | solution.py:315
  81.3 0.7 copy-start.13
  82.9 42.9 %copy-start.6 = (bf16[125,2048]{1,0:T(8,128)(2,1)S(1)}, bf16[125,2048]{1,0:T(8,128)(2,1)}, u32[]{:S(2)}) copy-start(bf16[125,2048]{1,0:T(8,128)(2,1)} %words_ref.1) | copy-start | bytes 1536004
  107.7 11.1 %copy-start.18 = (bf16[2048]{0:T(1024)(128)(2,1)S(1)}, bf16[2048]{0:T(1024)(128)(2,1)}, u32[]{:S(2)}) copy-start(bf16[2048]{0:T(1024)(128)(2,1)} %param.34) | copy-start | bytes 12292
  107.7 18.2 %all-to-all-start.6 = ((bf16[32,8,128]{2,1,0:T(8,128)(2,1)}), bf16[32,8,128]{2,1,0:T(8,128)(2,1)S(1)}, u32[]{:S(2)}, u32[]{:S(2)}) async-start(bf16[32,8,128]{2,1,0:T(8,128)(2,1)} %shard_map.187), calls=%async_computation.6 | async-start | bytes 131072 | tf_op jit(solution)/shard_map/all_to_all | solution.py:315
  118.7 7.1 %copy-start.14 = (s32[4]{0:T(128)S(1)}, s32[4]{0:T(128)}, u32[]{:S(2)}) copy-start(s32[4]{0:T(128)} %sizes_ref.1) | copy-start | bytes 52
  118.8 7.1 %copy-start.15 = (s32[4]{0:T(128)S(1)}, s32[4]{0:T(128)}, u32[]{:S(2)}) copy-start(s32[4]{0:T(128)} %guidance_ref.1) | copy-start | bytes 52

commit v2 on v1

--- a/solution.py
+++ b/solution.py
@@ -29,8 +29,8 @@
     return pl.BlockSpec(memory_space=pltpu.VMEM)
 
 
-def smem():
-    return pl.BlockSpec(memory_space=pltpu.SMEM)
+def hbm():
+    return pl.BlockSpec(memory_space=pltpu.HBM)
 
 
 def call(body, outs, specs, scratch=()):
@@ -74,10 +74,75 @@
     return jnp.sum(jnp.where(lanes == lane_of_row, share, 0.0), axis=1, keepdims=True)
 
 
+def guidance_factor(sizes_ref, guidance_ref, half):
+    request = lax.axis_index("cfg") * half + iota((half, 1), 0)
+    tenants = sizes_ref.shape[0]
+    tenant = jnp.zeros((half, 1), jnp.int32)
+    end = 0
+    for t in range(tenants):
+        end = end + sizes_ref[t]
+        tenant = tenant + (request >= end).astype(jnp.int32)
+    chosen = jnp.zeros((half, 1), jnp.int32)
+    for t in range(tenants):
+        chosen = jnp.where(tenant == t, guidance_ref[t], chosen)
+    return chosen.astype(F32) / 4.0
+
+
 def attend_kernel(
-    q_ref, k_ref, v_ref, new_ref, lengths_ref, ids_ref, out_ref, rows_ref
+    q_hbm,
+    k_hbm,
+    v_hbm,
+    new_hbm,
+    lengths_hbm,
+    ids_hbm,
+    sizes_hbm,
+    guidance_hbm,
+    out_ref,
+    factor_ref,
+    q_ref,
+    k_ref,
+    v_ref,
+    new_ref,
+    lengths_ref,
+    ids_ref,
+    sizes_ref,
+    guidance_ref,
+    rows_ref,
+    small_sems,
+    key_sems,
+    value_sems,
 ):
-    requests, positions = k_ref.shape[1], k_ref.shape[2]
+    requests, positions = k_ref.shape[0], k_ref.shape[1]
+    small = [
+        pltpu.make_async_copy(source, target, small_sems.at[n])
+        for n, (source, target) in enumerate(
+            [
+                (q_hbm, q_ref),
+                (new_hbm, new_ref),
+                (lengths_hbm, lengths_ref),
+                (ids_hbm, ids_ref),
+                (sizes_hbm, sizes_ref),
+                (guidance_hbm, guidance_ref),
+            ]
+        )
+    ]
+    keys = [
+        pltpu.make_async_copy(k_hbm.at[0, r], k_ref.at[r], key_sems.at[r]) for r in range(requests)
+    ]
+    values_in = [
+        pltpu.make_async_copy(v_hbm.at[0, r], v_ref.at[r], value_sems.at[r])
+        for r in range(requests)
+    ]
+    for copy in small:
+        copy.start()
+    for key, value in zip(keys, values_in):
+        key.start()
+        value.start()
+    for copy in small:
+        copy.wait()
+    factor_ref[...] = jnp.broadcast_to(
+        guidance_factor(sizes_ref, guidance_ref, factor_ref.shape[0]), factor_ref.shape
+    )
     block = lax.axis_index("z") * lax.axis_size("x") + lax.axis_index("x")
     first_request = lax.axis_index("req") * requests
     queries = q_ref[0].astype(F32)
@@ -93,8 +158,9 @@
             ],
             axis=0,
         )
+        keys[r].wait()
         scores = (
-            lax.dot_general(wide.astype(BF16), k_ref[0, r], NT, preferred_element_type=F32) * SCALE
+            lax.dot_general(wide.astype(BF16), k_ref[r], NT, preferred_element_type=F32) * SCALE
         )
         entry = new_ref[0, r].astype(F32)
         new_score = jnp.sum(wide * entry[0:1, :], axis=1, keepdims=True) * SCALE
@@ -108,7 +174,8 @@
         total = jnp.sum(weights, axis=1, keepdims=True) + fresh
         high = total.astype(BF16).astype(F32)
         low = total - high
-        values = dot(weights.astype(BF16), v_ref[0, r])
+        values_in[r].wait()
+        values = dot(weights.astype(BF16), v_ref[r])
         values = values + fresh.astype(BF16).astype(F32) * entry[1:2, :]
         for k in range(TOPK):
             for quarter in range(H // HEADS_ROW):
@@ -132,7 +199,7 @@
     for k in range(TOPK):
         picked = jnp.zeros((8, 1), jnp.int32)
         for r in range(requests):
-            picked = jnp.where(request == r, ids_ref[first_request + r, k], picked)
+            picked = jnp.where(request == r, ids_ref[k, first_request + r], picked)
         chosen.append(picked)
     for plane in range(out_ref.shape[0]):
         expert, half = plane // 2, plane % 2
@@ -172,7 +239,12 @@
     return numerator, denominator, peak
 
 
-def merge_kernel(in_ref, weight_ref, out_ref):
+def merge_kernel(
+    in_ref, weight_ref, first_gain_ref, second_gain_ref, ids_ref, out_ref, gains_ref, ids_out_ref
+):
+    gains_ref[0, :] = first_gain_ref[...].astype(F32)
+    gains_ref[1, :] = second_gain_ref[...].astype(F32)
+    ids_out_ref[...] = ids_ref[...]
     wide = HEADS_ROW * HD
     copies = out_ref.shape[0]
     stats = in_ref[:, :, wide:].astype(F32)[:, None]
@@ -257,7 +329,7 @@
         at = slice(chunk * LANES, (chunk + 1) * LANES)
         middle_ref[:, at] = residual_ref[0, :, at].astype(F32) + in_ref[chunk].astype(F32)
     middle = middle_ref[...]
-    inputs = (middle * rms(middle) * gain_ref[...].astype(F32)).astype(BF16)
+    inputs = (middle * rms(middle) * gain_ref[0:1, :]).astype(BF16)
     logits = lax.dot_general(router_ref[...], inputs, NT, preferred_element_type=F32)
     share = share_column(logits, ids_ref, expert_of_plane(), iota((requests, 1), 0))
     gate = lax.dot_general(inputs, gate_ref[...], NT, preferred_element_type=F32)
@@ -284,7 +356,7 @@
             out_ref[stream * copies + copy] = total[stream * half : (stream + 1) * half]
 
 
-def head_kernel(in_ref, gain_ref, words_ref, sizes_ref, guidance_ref, out_ref, joined_ref):
+def head_kernel(in_ref, gain_ref, words_ref, factor_ref, out_ref, joined_ref):
     half = in_ref.shape[1]
     chunks = in_ref.shape[0] // 2
     for stream in range(2):
@@ -294,19 +366,9 @@
                 stream * chunks + chunk
             ].astype(F32)
     joined = joined_ref[...]
-    inputs = (joined * rms(joined) * gain_ref[...].astype(F32)).astype(BF16)
+    inputs = (joined * rms(joined) * gain_ref[1:2, :]).astype(BF16)
     logits = lax.dot_general(inputs, words_ref[...], NT, preferred_element_type=F32)
-    request = lax.axis_index("cfg") * half + iota((half, 1), 0)
-    tenants = sizes_ref.shape[0]
-    tenant = jnp.zeros((half, 1), jnp.int32)
-    end = 0
-    for t in range(tenants):
-        end = end + sizes_ref[t]
-        tenant = tenant + (request >= end).astype(jnp.int32)
-    chosen = jnp.zeros((half, 1), jnp.int32)
-    for t in range(tenants):
-        chosen = jnp.where(tenant == t, guidance_ref[t], chosen)
-    factor = chosen.astype(F32) / 4.0
+    factor = factor_ref[:, :1]
     conditional, unconditional = logits[:half], logits[half:]
     out_ref[...] = unconditional + factor * (conditional - unconditional)
 
@@ -342,19 +404,53 @@
     requests = residual.shape[1]
     shape = jax.ShapeDtypeStruct
 
-    partial = call(
+    rows, positions = key_cache.shape[1:3]
+    partial, factor = call(
         attend_kernel,
-        shape((planes, 8, ROW), BF16),
-        [vmem()] * 4 + [smem()] * 2,
-        [pltpu.VMEM((2, TOPK, 8, ROW), F32)],
-    )(queries, key_cache, value_cache, new_entries, lengths, attention_ids)
+        (shape((planes, 8, ROW), BF16), shape((requests // 2, LANES), F32)),
+        [hbm()] * 8,
+        [
+            pltpu.VMEM(queries.shape, BF16),
+            pltpu.VMEM((rows, positions, D), BF16),
+            pltpu.VMEM((rows, positions, D), BF16),
+            pltpu.VMEM(new_entries.shape, BF16),
+            pltpu.SMEM(lengths.shape, jnp.int32),
+            pltpu.SMEM(attention_ids.shape[::-1], jnp.int32),
+            pltpu.SMEM(tenant_sizes.shape, jnp.int32),
+            pltpu.SMEM(guidance.shape, jnp.int32),
+            pltpu.VMEM((2, TOPK, 8, ROW), F32),
+            pltpu.SemaphoreType.DMA((6,)),
+            pltpu.SemaphoreType.DMA((rows,)),
+            pltpu.SemaphoreType.DMA((rows,)),
+        ],
+    )(
+        *(
+            pltpu.with_memory_space_constraint(operand, pltpu.HBM)
+            for operand in (
+                queries,
+                key_cache,
+                value_cache,
+                new_entries,
+                lengths,
+                attention_ids.T,
+                tenant_sizes,
+                guidance,
+            )
+        )
+    )
     partial = exchanged(partial, "z")
 
     weight_rows = attention_output.shape[0]
     merged_rows = HEADS_ROW * 8 + 8 + weight_rows
-    both = call(merge_kernel, shape((members, merged_rows, LANES), BF16), [vmem()] * 2)(
-        partial, attention_output
-    )
+    both, gains, ids = call(
+        merge_kernel,
+        (
+            shape((members, merged_rows, LANES), BF16),
+            shape((2, D), F32),
+            shape((TOPK, requests), jnp.int32),
+        ),
+        [vmem()] * 5,
+    )(partial, attention_output, expert_gain, final_gain, expert_ids.T)
     both = exchanged(both, plane)
 
     chunk = shape((planes, requests, LANES), BF16)
@@ -375,9 +471,9 @@
     )(
         attention,
         residual,
-        expert_gain[None],
+        gains,
         expert_router.T,
-        expert_ids.T,
+        ids,
         expert_gate,
         expert_up,
         expert_down,
@@ -395,9 +491,9 @@
     return call(
         head_kernel,
         shape((requests // 2, unembedding.shape[0]), F32),
-        [vmem()] * 3 + [smem()] * 2,
+        [vmem()] * 4,
         [pltpu.VMEM((requests, D), F32)],
-    )(final, final_gain[None], unembedding, tenant_sizes, guidance)
+    )(final, gains, unembedding, factor)
 
 
 def solution(mesh):

time: 128 us -> 122 us (0.953)
  blocking collectives: 86.1 us -> 114 us
  starting transfers between devices: 15.5 us -> 0 us
  waiting for transfers between devices: 13.6 us -> 0 us
  local copies, waits for them, and re-layouts: 5.29 us -> 0.72 us
    all_to_all x5 -> x7, blocking collectives: 86.1 us -> 114 us  [exchanged(): return lax.all_to_all(value, axis, 0, 0, tiled=True)]
    all_to_all x2 -> x0, starting transfers between devices: 15.5 us -> none  [exchanged(): return lax.all_to_all(value, axis, 0, 0, tiled=True)]
    all_to_all x2 -> x0, waiting for transfers between devices: 13.6 us -> none  [exchanged(): return lax.all_to_all(value, axis, 0, 0, tiled=True)]
    unnamed x39 -> x24, local copies, waits for them, and re-layouts: 5.27 us -> 0.72 us
    pallas_call x2, Pallas kernels: 2.38 us -> 3.81 us  [the longest x1 3.51 us: local(): call(attend_kernel, (shape((planes, 8, ROW), BF16), shape((requests // 2,...]
  transfers between devices with their start and end apart: 2 -> 0, of which waited for: 2 -> 0; matrix products, arithmetic and copies ran while one was open for 0% -> 0% of each run, Pallas kernels for 0% -> 0%
where the time goes in v2:
time: 122 us
  blocking collectives  114 us (93%)
  Pallas kernels  6.36 us (5%)
    all_to_all x7, blocking collectives, exchanged(): return lax.all_to_all(value, axis, 0, 0, tiled=True)  114 us
    pallas_call x1, Pallas kernels, local(): call(attend_kernel, (shape((planes, 8, ROW), BF16), shape((requests // 2,...  3.51 us

profile of v2, /device:TPU:1, one launch (start us, length us, event | category | flops | bytes accessed | tf_op | source)
XLA Modules:
  0.0 121.7 jit_solution(13545251345410474849)
XLA Ops:
  0.0 3.5 %shard_map.181 = (bf16[16,8,640]{2,1,0:T(8,128)(2,1)S(1)}, f32[8,128]{1,0:T(8,128)S(1)}) custom-call(bf16[1,4,4096]{2,1,0:T(4,128)(2,1)} %q_hbm.1, bf16[1,4,48,2048]{3,2,1,0:T(8,128)(2,1)} %k_hbm.1, bf16[1,4,48,2048]{3,2,1,0:T(8,128)(2,1)} %v_hbm.1, bf16[1,4,2,2048]{3,2,1,0:T(2,128)(2,1)} %new_hbm.1, s32[1,4]{1,0:T(1,128)} %lengths_hbm.1, s32[2,16]{1,0:T(2,128)} %bitcast.6, ...), custom_call_target="tpu_custom_call" | custom-call | tf_op jit(solution)/shard_map/pallas_call | solution.py:408
  3.5 0.0 copy-start.5
  3.5 0.0 copy-start.8
  3.5 0.0 copy-start.9
  3.6 0.0 copy-start.7
  3.6 27.9 %all_to_all.35.in_ref = bf16[16,8,640]{2,1,0:T(8,128)(2,1)S(1)} all-to-all(bf16[16,8,640]{2,1,0:T(8,128)(2,1)S(1)} %get-tuple-element.10), channel_id=1, replica_groups=mesh['cfg'=2,'z'=16,'x'=4,'req'=4] {'z'}, dimensions={0} | all-to-all | bytes 327680 | tf_op jit(solution)/shard_map/all_to_all | solution.py:377
  31.5 0.0 copy-done.5
  31.5 0.0 copy-done.9
  31.5 0.7 copy-done.11
  32.2 0.3 shard_map.182
  32.5 0.0 copy-start
  32.5 0.0 copy-start.1
  32.5 14.8 %all_to_all.36.in_ref = bf16[16,104,128]{2,1,0:T(8,128)(2,1)S(1)} all-to-all(bf16[16,104,128]{2,1,0:T(8,128)(2,1)S(1)} %get-tuple-element.11), channel_id=1, replica_groups=mesh['cfg'=2,'z'=16,'x'=4,'req'=4] {'x','req'}, dimensions={0} | all-to-all | bytes 851968 | tf_op jit(solution)/shard_map/all_to_all | solution.py:377
  47.3 0.0 copy-done.10
  47.3 0.6 shard_map.183
  47.9 19.4 %all_to_all.37.in_ref.attention_ref = bf16[16,16,128]{2,1,0:T(8,128)(2,1)S(1)} all-to-all(bf16[16,16,128]{2,1,0:T(8,128)(2,1)S(1)} %shard_map.183), channel_id=1, replica_groups=mesh['cfg'=2,'z'=16,'x'=4,'req'=4] {'z'}, dimensions={0} | all-to-all | bytes 131072 | tf_op jit(solution)/shard_map/all_to_all | solution.py:377
  67.3 10.6 %all_to_all.38.in_ref = bf16[16,16,128]{2,1,0:T(8,128)(2,1)S(1)} all-to-all(bf16[16,16,128]{2,1,0:T(8,128)(2,1)S(1)} %shard_map.184), channel_id=1, replica_groups=mesh['cfg'=2,'z'=16,'x'=4,'req'=4] {'x','req'}, dimensions={0} | all-to-all | bytes 131072 | tf_op jit(solution)/shard_map/all_to_all | solution.py:377
  77.9 0.0 copy-done.1
  77.9 0.0 copy-done.6
  77.9 0.9 shard_map.185
  78.9 9.6 %all_to_all.39.in_ref = bf16[16,16,128]{2,1,0:T(8,128)(2,1)S(1)} all-to-all(bf16[16,16,128]{2,1,0:T(8,128)(2,1)S(1)} %shard_map.185), channel_id=1, replica_groups=mesh['cfg'=2,'z'=16,'x'=4,'req'=4] {'x','req'}, dimensions={0} | all-to-all | bytes 131072 | tf_op jit(solution)/shard_map/all_to_all | solution.py:377
  88.5 14.4 %all_to_all.40.in_ref = bf16[16,16,128]{2,1,0:T(8,128)(2,1)S(1)} all-to-all(bf16[16,16,128]{2,1,0:T(8,128)(2,1)S(1)} %shard_map.186), channel_id=1, replica_groups=mesh['cfg'=2,'z'=16,'x'=4,'req'=4] {'z'}, dimensions={0} | all-to-all | bytes 131072 | tf_op jit(solution)/shard_map/all_to_all | solution.py:377
  103.0 17.8 %all_to_all.41.in_ref = bf16[32,8,128]{2,1,0:T(8,128)(2,1)S(1)} all-to-all(bf16[32,8,128]{2,1,0:T(8,128)(2,1)S(1)} %shard_map.187), channel_id=1, replica_groups=mesh['cfg'=2,'z'=16,'x'=4,'req'=4] {'cfg','x','req'}, dimensions={0} | all-to-all | bytes 131072 | tf_op jit(solution)/shard_map/all_to_all | solution.py:377
  120.8 0.9 shard_map.188
  (15 shorter events, 0.1 us)
Async XLA Ops:
  3.5 27.9 %copy-start.5 = (bf16[64,2048]{1,0:T(8,128)(2,1)S(1)}, bf16[64,2048]{1,0:T(8,128)(2,1)}, u32[]{:S(2)}) copy-start(bf16[64,2048]{1,0:T(8,128)(2,1)} %weight_ref.1) | copy-start | bytes 786436
  3.5 27.9 %copy-start.8 = (bf16[2048]{0:T(1024)(128)(2,1)S(1)}, bf16[2048]{0:T(1024)(128)(2,1)}, u32[]{:S(2)}) copy-start(bf16[2048]{0:T(1024)(128)(2,1)} %first_gain_ref.1) | copy-start | bytes 12292
  3.5 27.9 %copy-start.9 = (bf16[2048]{0:T(1024)(128)(2,1)S(1)}, bf16[2048]{0:T(1024)(128)(2,1)}, u32[]{:S(2)}) copy-start(bf16[2048]{0:T(1024)(128)(2,1)} %second_gain_ref.1) | copy-start | bytes 12292
  3.6 43.7 %copy-start.7 = (bf16[2048,8]{0,1:T(8,128)(2,1)S(1)}, bf16[2048,8]{0,1:T(8,128)(2,1)}, u32[]{:S(2)}) copy-start(bf16[2048,8]{0,1:T(8,128)(2,1)} %param.27) | copy-start | bytes 98308
  31.5 0.7 copy-start.11
  32.1 15.2 %copy-start.3 = (bf16[1,16,2048]{2,1,0:T(8,128)(2,1)S(1)}, bf16[1,16,2048]{2,1,0:T(8,128)(2,1)}, u32[]{:S(2)}) copy-start(bf16[1,16,2048]{2,1,0:T(8,128)(2,1)} %residual_ref.5) | copy-start | bytes 196612
  32.1 15.2 %copy-start.10 = (s32[16,2]{0,1:T(2,128)S(1)}, s32[16,2]{0,1:T(2,128)}, u32[]{:S(2)}) copy-start(s32[16,2]{0,1:T(2,128)} %param.25) | copy-start | bytes 388
  32.1 45.8 %copy-start.2 = (bf16[176,2048]{1,0:T(8,128)(2,1)S(1)}, bf16[176,2048]{1,0:T(8,128)(2,1)}, u32[]{:S(2)}) copy-start(bf16[176,2048]{1,0:T(8,128)(2,1)} %down_ref.1) | copy-start | bytes 2162692
  32.5 45.5 %copy-start = (bf16[176,2048]{1,0:T(8,128)(2,1)S(1)}, bf16[176,2048]{1,0:T(8,128)(2,1)}, u32[]{:S(2)}) copy-start(bf16[176,2048]{1,0:T(8,128)(2,1)} %gate_ref.1) | copy-start | bytes 2162692
  32.5 45.5 %copy-start.1 = (bf16[176,2048]{1,0:T(8,128)(2,1)S(1)}, bf16[176,2048]{1,0:T(8,128)(2,1)}, u32[]{:S(2)}) copy-start(bf16[176,2048]{1,0:T(8,128)(2,1)} %up_ref.1) | copy-start | bytes 2162692
  67.3 10.6 %copy-start.6 = (bf16[2048,8]{0,1:T(8,128)(2,1)S(1)}, bf16[2048,8]{0,1:T(8,128)(2,1)}, u32[]{:S(2)}) copy-start(bf16[2048,8]{0,1:T(8,128)(2,1)} %param.28) | copy-start | bytes 98308
  78.9 41.9 %copy-start.4 = (bf16[125,2048]{1,0:T(8,128)(2,1)S(1)}, bf16[125,2048]{1,0:T(8,128)(2,1)}, u32[]{:S(2)}) copy-start(bf16[125,2048]{1,0:T(8,128)(2,1)} %words_ref.1) | copy-start | bytes 1536004

commit v3 on v2

--- a/solution.py
+++ b/solution.py
@@ -15,6 +15,7 @@
 TOPK = 2
 EPS = 1e-05
 NEG = -1e30
+SPARE = 8
 LANES = 128
 HEADS_ROW = 4
 ROW = HEADS_ROW * HD + LANES
@@ -97,8 +98,10 @@
     ids_hbm,
     sizes_hbm,
     guidance_hbm,
+    expert_ids_hbm,
     out_ref,
     factor_ref,
+    expert_ids_ref,
     q_ref,
     k_ref,
     v_ref,
@@ -112,7 +115,7 @@
     key_sems,
     value_sems,
 ):
-    requests, positions = k_ref.shape[0], k_ref.shape[1]
+    requests, positions = k_hbm.shape[1], k_hbm.shape[2]
     small = [
         pltpu.make_async_copy(source, target, small_sems.at[n])
         for n, (source, target) in enumerate(
@@ -123,14 +126,16 @@
                 (ids_hbm, ids_ref),
                 (sizes_hbm, sizes_ref),
                 (guidance_hbm, guidance_ref),
+                (expert_ids_hbm, expert_ids_ref),
             ]
         )
     ]
     keys = [
-        pltpu.make_async_copy(k_hbm.at[0, r], k_ref.at[r], key_sems.at[r]) for r in range(requests)
+        pltpu.make_async_copy(k_hbm.at[0, r], k_ref.at[r, :positions], key_sems.at[r])
+        for r in range(requests)
     ]
     values_in = [
-        pltpu.make_async_copy(v_hbm.at[0, r], v_ref.at[r], value_sems.at[r])
+        pltpu.make_async_copy(v_hbm.at[0, r], v_ref.at[r, :positions], value_sems.at[r])
         for r in range(requests)
     ]
     for copy in small:
@@ -138,16 +143,30 @@
     for key, value in zip(keys, values_in):
         key.start()
         value.start()
+    block = lax.axis_index("z") * lax.axis_size("x") + lax.axis_index("x")
+    owner = block == 0
+    v_ref[:, positions:, :] = jnp.zeros((requests, SPARE, D), BF16)
     for copy in small:
         copy.wait()
+
+    @pl.when(owner)
+    def _():
+        for r in range(requests):
+            entry = new_ref[0, r].astype(F32)
+            first = iota((SPARE, D), 0) == 0
+            k_ref[r, positions:, :] = jnp.where(first, entry[0:1, :], 0.0).astype(BF16)
+            v_ref[r, positions:, :] = jnp.where(first, entry[1:2, :], 0.0).astype(BF16)
+
     factor_ref[...] = jnp.broadcast_to(
         guidance_factor(sizes_ref, guidance_ref, factor_ref.shape[0]), factor_ref.shape
     )
-    block = lax.axis_index("z") * lax.axis_size("x") + lax.axis_index("x")
     first_request = lax.axis_index("req") * requests
     queries = q_ref[0].astype(F32)
     own_head = iota((H, D), 0) == iota((H, D), 1) // HD
-    place = block * positions + iota((1, positions), 1)
+    column = iota((1, positions + SPARE), 1)
+    place = block * positions + column
+    cached = column < positions
+    fresh = (column == positions) & owner
     sub = iota((8, LANES), 0)
     lane = iota((8, LANES), 1)
     for r in range(requests):
@@ -162,21 +181,15 @@
         scores = (
             lax.dot_general(wide.astype(BF16), k_ref[r], NT, preferred_element_type=F32) * SCALE
         )
-        entry = new_ref[0, r].astype(F32)
-        new_score = jnp.sum(wide * entry[0:1, :], axis=1, keepdims=True) * SCALE
-        live = place < lengths_ref[0, r]
-        owner = block == 0
+        live = (cached & (place < lengths_ref[0, r])) | fresh
         top = jnp.max(jnp.where(live, scores, NEG), axis=1, keepdims=True)
-        top = jnp.maximum(top, jnp.where(owner, new_score, NEG))
         peak = top.astype(BF16).astype(F32)
         weights = jnp.where(live, jnp.exp(scores - peak), 0.0)
-        fresh = jnp.where(owner, jnp.exp(new_score - peak), 0.0)
-        total = jnp.sum(weights, axis=1, keepdims=True) + fresh
+        total = jnp.sum(weights, axis=1, keepdims=True)
         high = total.astype(BF16).astype(F32)
         low = total - high
         values_in[r].wait()
         values = dot(weights.astype(BF16), v_ref[r])
-        values = values + fresh.astype(BF16).astype(F32) * entry[1:2, :]
         for k in range(TOPK):
             for quarter in range(H // HEADS_ROW):
                 half, group = quarter // 2, quarter % 2
@@ -186,11 +199,11 @@
                     head = quarter * HEADS_ROW + j
                     tile = values[base : base + 8, head * HD : (head + 1) * HD]
                     parts.append(jnp.sum(jnp.where(sub == head % 8, tile, 0.0), axis=0, keepdims=True))
-                column = sub - group * HEADS_ROW
-                here = (column >= 0) & (column < HEADS_ROW)
-                stats = jnp.where(lane == column, peak[base : base + 8], 0.0)
-                stats = stats + jnp.where(lane == column + 4, high[base : base + 8], 0.0)
-                stats = stats + jnp.where(lane == column + 8, low[base : base + 8], 0.0)
+                part = sub - group * HEADS_ROW
+                here = (part >= 0) & (part < HEADS_ROW)
+                stats = jnp.where(lane == part, peak[base : base + 8], 0.0)
+                stats = stats + jnp.where(lane == part + 4, high[base : base + 8], 0.0)
+                stats = stats + jnp.where(lane == part + 8, low[base : base + 8], 0.0)
                 parts.append(jnp.sum(jnp.where(here, stats, 0.0), axis=0, keepdims=True))
                 row = group * requests + r
                 rows_ref[half, k, row : row + 1, :] = jnp.concatenate(parts, axis=1)
@@ -240,11 +253,10 @@
 
 
 def merge_kernel(
-    in_ref, weight_ref, first_gain_ref, second_gain_ref, ids_ref, out_ref, gains_ref, ids_out_ref
+    in_ref, weight_ref, first_gain_ref, second_gain_ref, out_ref, gains_ref
 ):
     gains_ref[0, :] = first_gain_ref[...].astype(F32)
     gains_ref[1, :] = second_gain_ref[...].astype(F32)
-    ids_out_ref[...] = ids_ref[...]
     wide = HEADS_ROW * HD
     copies = out_ref.shape[0]
     stats = in_ref[:, :, wide:].astype(F32)[:, None]
@@ -405,21 +417,25 @@
     shape = jax.ShapeDtypeStruct
 
     rows, positions = key_cache.shape[1:3]
-    partial, factor = call(
+    partial, factor, ids = call(
         attend_kernel,
-        (shape((planes, 8, ROW), BF16), shape((requests // 2, LANES), F32)),
-        [hbm()] * 8,
+        (
+            shape((planes, 8, ROW), BF16),
+            shape((requests // 2, LANES), F32),
+            shape(expert_ids.shape[::-1], jnp.int32),
+        ),
+        [hbm()] * 9,
         [
             pltpu.VMEM(queries.shape, BF16),
-            pltpu.VMEM((rows, positions, D), BF16),
-            pltpu.VMEM((rows, positions, D), BF16),
+            pltpu.VMEM((rows, positions + SPARE, D), BF16),
+            pltpu.VMEM((rows, positions + SPARE, D), BF16),
             pltpu.VMEM(new_entries.shape, BF16),
             pltpu.SMEM(lengths.shape, jnp.int32),
             pltpu.SMEM(attention_ids.shape[::-1], jnp.int32),
             pltpu.SMEM(tenant_sizes.shape, jnp.int32),
             pltpu.SMEM(guidance.shape, jnp.int32),
             pltpu.VMEM((2, TOPK, 8, ROW), F32),
-            pltpu.SemaphoreType.DMA((6,)),
+            pltpu.SemaphoreType.DMA((7,)),
             pltpu.SemaphoreType.DMA((rows,)),
             pltpu.SemaphoreType.DMA((rows,)),
         ],
@@ -435,6 +451,7 @@
                 attention_ids.T,
                 tenant_sizes,
                 guidance,
+                expert_ids.T,
             )
         )
     )
@@ -442,15 +459,11 @@
 
     weight_rows = attention_output.shape[0]
     merged_rows = HEADS_ROW * 8 + 8 + weight_rows
-    both, gains, ids = call(
+    both, gains = call(
         merge_kernel,
-        (
-            shape((members, merged_rows, LANES), BF16),
-            shape((2, D), F32),
-            shape((TOPK, requests), jnp.int32),
-        ),
-        [vmem()] * 5,
-    )(partial, attention_output, expert_gain, final_gain, expert_ids.T)
+        (shape((members, merged_rows, LANES), BF16), shape((2, D), F32)),
+        [vmem()] * 4,
+    )(partial, attention_output, expert_gain, final_gain)
     both = exchanged(both, plane)
 
     chunk = shape((planes, requests, LANES), BF16)

time: 122 us -> 122 us (level)
  no operation moved by 1% of the time
where the time goes in v3:
time: 122 us; the launch traced here: 121 us
  blocking collectives  114 us (93%)
  Pallas kernels  6.86 us (6%)
    all_to_all x7, blocking collectives, exchanged(): return lax.all_to_all(value, axis, 0, 0, tiled=True)  114 us
    pallas_call x1, Pallas kernels, local(): call(attend_kernel, (shape((planes, 8, ROW), BF16), shape((requests // 2,...  4.01 us

profile of v3, /device:TPU:1, one launch (start us, length us, event | category | flops | bytes accessed | tf_op | source)
XLA Modules:
  0.0 121.5 jit_solution(17523198824037333075)
XLA Ops:
  0.0 4.0 %shard_map.181 = (bf16[16,8,640]{2,1,0:T(8,128)(2,1)S(1)}, f32[8,128]{1,0:T(8,128)S(1)}, s32[2,16]{1,0:T(2,128)S(1)}) custom-call(bf16[1,4,4096]{2,1,0:T(4,128)(2,1)} %q_hbm.1, bf16[1,4,48,2048]{3,2,1,0:T(8,128)(2,1)} %k_hbm.1, bf16[1,4,48,2048]{3,2,1,0:T(8,128)(2,1)} %v_hbm.1, bf16[1,4,2,2048]{3,2,1,0:T(2,128)(2,1)} %new_hbm.1, s32[1,4]{1,0:T(1,128)} %lengths_hbm.1, ...), custom_call_target="tpu_custom_call" | custom-call | tf_op jit(solution)/shard_map/pallas_call | solution.py:420
  4.0 0.0 copy-start.5
  4.0 0.0 copy-start.8
  4.0 0.0 copy-start.9
  4.1 0.0 copy-start.7
  4.1 27.8 %all_to_all.35.in_ref = bf16[16,8,640]{2,1,0:T(8,128)(2,1)S(1)} all-to-all(bf16[16,8,640]{2,1,0:T(8,128)(2,1)S(1)} %get-tuple-element.10), channel_id=1, replica_groups=mesh['cfg'=2,'z'=16,'x'=4,'req'=4] {'z'}, dimensions={0} | all-to-all | bytes 327680 | tf_op jit(solution)/shard_map/all_to_all | solution.py:389
  31.9 0.0 copy-done.9
  31.9 0.0 copy-start.3
  31.9 0.0 copy-start.10
  31.9 0.0 copy-start.2
  31.9 0.3 shard_map.182
  32.3 0.0 copy-start
  32.3 0.0 copy-start.1
  32.3 14.8 %all_to_all.36.in_ref = bf16[16,104,128]{2,1,0:T(8,128)(2,1)S(1)} all-to-all(bf16[16,104,128]{2,1,0:T(8,128)(2,1)S(1)} %get-tuple-element.11), channel_id=1, replica_groups=mesh['cfg'=2,'z'=16,'x'=4,'req'=4] {'x','req'}, dimensions={0} | all-to-all | bytes 851968 | tf_op jit(solution)/shard_map/all_to_all | solution.py:389
  47.1 0.0 copy-done.10
  47.1 0.6 shard_map.183
  47.7 19.4 %all_to_all.37.in_ref.attention_ref = bf16[16,16,128]{2,1,0:T(8,128)(2,1)S(1)} all-to-all(bf16[16,16,128]{2,1,0:T(8,128)(2,1)S(1)} %shard_map.183), channel_id=1, replica_groups=mesh['cfg'=2,'z'=16,'x'=4,'req'=4] {'z'}, dimensions={0} | all-to-all | bytes 131072 | tf_op jit(solution)/shard_map/all_to_all | solution.py:389
  67.1 10.6 %all_to_all.38.in_ref = bf16[16,16,128]{2,1,0:T(8,128)(2,1)S(1)} all-to-all(bf16[16,16,128]{2,1,0:T(8,128)(2,1)S(1)} %shard_map.184), channel_id=1, replica_groups=mesh['cfg'=2,'z'=16,'x'=4,'req'=4] {'x','req'}, dimensions={0} | all-to-all | bytes 131072 | tf_op jit(solution)/shard_map/all_to_all | solution.py:389
  77.7 0.0 copy-done.6
  77.7 0.9 shard_map.185
  78.7 9.6 %all_to_all.39.in_ref = bf16[16,16,128]{2,1,0:T(8,128)(2,1)S(1)} all-to-all(bf16[16,16,128]{2,1,0:T(8,128)(2,1)S(1)} %shard_map.185), channel_id=1, replica_groups=mesh['cfg'=2,'z'=16,'x'=4,'req'=4] {'x','req'}, dimensions={0} | all-to-all | bytes 131072 | tf_op jit(solution)/shard_map/all_to_all | solution.py:389
  88.3 14.4 %all_to_all.40.in_ref = bf16[16,16,128]{2,1,0:T(8,128)(2,1)S(1)} all-to-all(bf16[16,16,128]{2,1,0:T(8,128)(2,1)S(1)} %shard_map.186), channel_id=1, replica_groups=mesh['cfg'=2,'z'=16,'x'=4,'req'=4] {'z'}, dimensions={0} | all-to-all | bytes 131072 | tf_op jit(solution)/shard_map/all_to_all | solution.py:389
  102.8 17.8 %all_to_all.41.in_ref = bf16[32,8,128]{2,1,0:T(8,128)(2,1)S(1)} all-to-all(bf16[32,8,128]{2,1,0:T(8,128)(2,1)S(1)} %shard_map.187), channel_id=1, replica_groups=mesh['cfg'=2,'z'=16,'x'=4,'req'=4] {'cfg','x','req'}, dimensions={0} | all-to-all | bytes 131072 | tf_op jit(solution)/shard_map/all_to_all | solution.py:389
  120.6 0.9 shard_map.188
  (13 shorter events, 0.1 us)
Async XLA Ops:
  4.0 27.9 %copy-start.5 = (bf16[64,2048]{1,0:T(8,128)(2,1)S(1)}, bf16[64,2048]{1,0:T(8,128)(2,1)}, u32[]{:S(2)}) copy-start(bf16[64,2048]{1,0:T(8,128)(2,1)} %weight_ref.1) | copy-start | bytes 786436
  4.0 27.9 %copy-start.8 = (bf16[2048]{0:T(1024)(128)(2,1)S(1)}, bf16[2048]{0:T(1024)(128)(2,1)}, u32[]{:S(2)}) copy-start(bf16[2048]{0:T(1024)(128)(2,1)} %first_gain_ref.1) | copy-start | bytes 12292
  4.0 27.9 %copy-start.9 = (bf16[2048]{0:T(1024)(128)(2,1)S(1)}, bf16[2048]{0:T(1024)(128)(2,1)}, u32[]{:S(2)}) copy-start(bf16[2048]{0:T(1024)(128)(2,1)} %second_gain_ref.1) | copy-start | bytes 12292
  4.1 43.0 %copy-start.7 = (bf16[2048,8]{0,1:T(8,128)(2,1)S(1)}, bf16[2048,8]{0,1:T(8,128)(2,1)}, u32[]{:S(2)}) copy-start(bf16[2048,8]{0,1:T(8,128)(2,1)} %param.27) | copy-start | bytes 98308
  31.9 15.2 %copy-start.3 = (bf16[1,16,2048]{2,1,0:T(8,128)(2,1)S(1)}, bf16[1,16,2048]{2,1,0:T(8,128)(2,1)}, u32[]{:S(2)}) copy-start(bf16[1,16,2048]{2,1,0:T(8,128)(2,1)} %residual_ref.5) | copy-start | bytes 196612
  31.9 15.2 %copy-start.10 = (s32[16,2]{0,1:T(2,128)S(1)}, s32[16,2]{0,1:T(2,128)}, u32[]{:S(2)}) copy-start(s32[16,2]{0,1:T(2,128)} %param.25) | copy-start | bytes 388
  31.9 45.8 %copy-start.2 = (bf16[176,2048]{1,0:T(8,128)(2,1)S(1)}, bf16[176,2048]{1,0:T(8,128)(2,1)}, u32[]{:S(2)}) copy-start(bf16[176,2048]{1,0:T(8,128)(2,1)} %down_ref.1) | copy-start | bytes 2162692
  32.3 45.5 %copy-start = (bf16[176,2048]{1,0:T(8,128)(2,1)S(1)}, bf16[176,2048]{1,0:T(8,128)(2,1)}, u32[]{:S(2)}) copy-start(bf16[176,2048]{1,0:T(8,128)(2,1)} %gate_ref.1) | copy-start | bytes 2162692
  32.3 45.5 %copy-start.1 = (bf16[176,2048]{1,0:T(8,128)(2,1)S(1)}, bf16[176,2048]{1,0:T(8,128)(2,1)}, u32[]{:S(2)}) copy-start(bf16[176,2048]{1,0:T(8,128)(2,1)} %up_ref.1) | copy-start | bytes 2162692
  67.1 10.6 %copy-start.6 = (bf16[2048,8]{0,1:T(8,128)(2,1)S(1)}, bf16[2048,8]{0,1:T(8,128)(2,1)}, u32[]{:S(2)}) copy-start(bf16[2048,8]{0,1:T(8,128)(2,1)} %param.28) | copy-start | bytes 98308
  78.7 41.9 %copy-start.4 = (bf16[125,2048]{1,0:T(8,128)(2,1)S(1)}, bf16[125,2048]{1,0:T(8,128)(2,1)}, u32[]{:S(2)}) copy-start(bf16[125,2048]{1,0:T(8,128)(2,1)} %words_ref.1) | copy-start | bytes 1536004

commit v4 on v3

--- a/solution.py
+++ b/solution.py
@@ -15,7 +15,7 @@
 TOPK = 2
 EPS = 1e-05
 NEG = -1e30
-SPARE = 8
+SPARE = 16
 LANES = 128
 HEADS_ROW = 4
 ROW = HEADS_ROW * HD + LANES
@@ -138,58 +138,72 @@
         pltpu.make_async_copy(v_hbm.at[0, r], v_ref.at[r, :positions], value_sems.at[r])
         for r in range(requests)
     ]
-    for copy in small:
+    small[0].start()
+    for key in keys:
+        key.start()
+    for copy in small[1:]:
         copy.start()
-    for key, value in zip(keys, values_in):
-        key.start()
+    for value in values_in:
         value.start()
     block = lax.axis_index("z") * lax.axis_size("x") + lax.axis_index("x")
     owner = block == 0
-    v_ref[:, positions:, :] = jnp.zeros((requests, SPARE, D), BF16)
-    for copy in small:
-        copy.wait()
-
-    @pl.when(owner)
-    def _():
-        for r in range(requests):
-            entry = new_ref[0, r].astype(F32)
-            first = iota((SPARE, D), 0) == 0
-            k_ref[r, positions:, :] = jnp.where(first, entry[0:1, :], 0.0).astype(BF16)
-            v_ref[r, positions:, :] = jnp.where(first, entry[1:2, :], 0.0).astype(BF16)
-
-    factor_ref[...] = jnp.broadcast_to(
-        guidance_factor(sizes_ref, guidance_ref, factor_ref.shape[0]), factor_ref.shape
-    )
     first_request = lax.axis_index("req") * requests
+    own_head = iota((H, D), 0) == iota((H, D), 1) // HD
+    small[0].wait()
     queries = q_ref[0].astype(F32)
-    own_head = iota((H, D), 0) == iota((H, D), 1) // HD
-    column = iota((1, positions + SPARE), 1)
-    place = block * positions + column
-    cached = column < positions
-    fresh = (column == positions) & owner
-    sub = iota((8, LANES), 0)
-    lane = iota((8, LANES), 1)
-    for r in range(requests):
-        wide = jnp.concatenate(
+    wide = [
+        jnp.concatenate(
             [
                 jnp.where(own_head, queries[r : r + 1, k * D : (k + 1) * D], 0.0)
                 for k in range(TOPK)
             ],
             axis=0,
-        )
-        keys[r].wait()
-        scores = (
-            lax.dot_general(wide.astype(BF16), k_ref[r], NT, preferred_element_type=F32) * SCALE
-        )
-        live = (cached & (place < lengths_ref[0, r])) | fresh
-        top = jnp.max(jnp.where(live, scores, NEG), axis=1, keepdims=True)
-        peak = top.astype(BF16).astype(F32)
-        weights = jnp.where(live, jnp.exp(scores - peak), 0.0)
-        total = jnp.sum(weights, axis=1, keepdims=True)
-        high = total.astype(BF16).astype(F32)
-        low = total - high
-        values_in[r].wait()
-        values = dot(weights.astype(BF16), v_ref[r])
+        ).astype(BF16)
+        for r in range(requests)
+    ]
+    for copy in small[1:]:
+        copy.wait()
+    new_row = (iota((SPARE, D), 0) == 0) & owner
+    for r in range(requests):
+        entry = new_ref[0, r].astype(F32)
+        k_ref[r, positions:, :] = jnp.where(new_row, entry[0:1, :], 0.0).astype(BF16)
+        v_ref[r, positions:, :] = jnp.where(new_row, entry[1:2, :], 0.0).astype(BF16)
+    factor_ref[...] = jnp.broadcast_to(
+        guidance_factor(sizes_ref, guidance_ref, factor_ref.shape[0]), factor_ref.shape
+    )
+    for key in keys:
+        key.wait()
+    scores = jnp.concatenate(
+        [
+            lax.dot_general(wide[r], k_ref[r], NT, preferred_element_type=F32)
+            for r in range(requests)
+        ],
+        axis=0,
+    )
+    scores = scores * SCALE
+    heads = TOPK * H
+    request_of_row = iota((requests * heads, 1), 0) // heads
+    length = jnp.zeros((requests * heads, 1), jnp.int32)
+    for r in range(requests):
+        length = jnp.where(request_of_row == r, lengths_ref[0, r], length)
+    column = iota(scores.shape, 1)
+    live = (column < positions) & (block * positions + column < length)
+    live = live | ((column == positions) & owner)
+    top = jnp.max(jnp.where(live, scores, NEG), axis=1, keepdims=True)
+    peaks = top.astype(BF16).astype(F32)
+    weights = jnp.where(live, jnp.exp(scores - peaks), 0.0)
+    totals = jnp.sum(weights, axis=1, keepdims=True)
+    highs = totals.astype(BF16).astype(F32)
+    lows = totals - highs
+    weights = weights.astype(BF16)
+    for value in values_in:
+        value.wait()
+    products = [dot(weights[r * heads : (r + 1) * heads], v_ref[r]) for r in range(requests)]
+    sub = iota((8, LANES), 0)
+    lane = iota((8, LANES), 1)
+    for r in range(requests):
+        at = slice(r * heads, (r + 1) * heads)
+        values, peak, high, low = products[r], peaks[at], highs[at], lows[at]
         for k in range(TOPK):
             for quarter in range(H // HEADS_ROW):
                 half, group = quarter // 2, quarter % 2

time: 122 us -> 121 us (level)
  Pallas kernels: 6.86 us -> 5.4 us
    pallas_call x1, Pallas kernels: 4.01 us -> 2.55 us  [local(): call(attend_kernel, (shape((planes, 8, ROW), BF16), shape((requests // 2,...]
where the time goes in v4:
time: 121 us; the launch traced here: 120 us
  blocking collectives  115 us (95%)
  Pallas kernels  5.4 us (4%)
    all_to_all x7, blocking collectives, exchanged(): return lax.all_to_all(value, axis, 0, 0, tiled=True)  115 us
    pallas_call x1, Pallas kernels, local(): call(attend_kernel, (shape((planes, 8, ROW), BF16), shape((requests // 2,...  2.55 us

profile of v4, /device:TPU:1, one launch (start us, length us, event | category | flops | bytes accessed | tf_op | source)
XLA Modules:
  0.0 120.1 jit_solution(5843745764557370629)
XLA Ops:
  0.0 2.5 %shard_map.181 = (bf16[16,8,640]{2,1,0:T(8,128)(2,1)S(1)}, f32[8,128]{1,0:T(8,128)S(1)}, s32[2,16]{1,0:T(2,128)S(1)}) custom-call(bf16[1,4,4096]{2,1,0:T(4,128)(2,1)} %q_hbm.1, bf16[1,4,48,2048]{3,2,1,0:T(8,128)(2,1)} %k_hbm.1, bf16[1,4,48,2048]{3,2,1,0:T(8,128)(2,1)} %v_hbm.1, bf16[1,4,2,2048]{3,2,1,0:T(2,128)(2,1)} %new_hbm.1, s32[1,4]{1,0:T(1,128)} %lengths_hbm.1, ...), custom_call_target="tpu_custom_call" | custom-call | tf_op jit(solution)/shard_map/pallas_call | solution.py:434
  2.6 0.0 copy-start.5
  2.6 0.0 copy-start.8
  2.6 0.0 copy-start.9
  2.6 0.0 copy-start.7
  2.6 27.9 %all_to_all.35.in_ref = bf16[16,8,640]{2,1,0:T(8,128)(2,1)S(1)} all-to-all(bf16[16,8,640]{2,1,0:T(8,128)(2,1)S(1)} %get-tuple-element.10), channel_id=1, replica_groups=mesh['cfg'=2,'z'=16,'x'=4,'req'=4] {'z'}, dimensions={0} | all-to-all | bytes 327680 | tf_op jit(solution)/shard_map/all_to_all | solution.py:403
  30.5 0.0 copy-done.9
  30.5 0.0 copy-start.3
  30.5 0.0 copy-start.10
  30.5 0.0 copy-start.2
  30.6 0.3 shard_map.182
  30.9 0.0 copy-start
  30.9 0.0 copy-start.1
  30.9 14.8 %all_to_all.36.in_ref = bf16[16,104,128]{2,1,0:T(8,128)(2,1)S(1)} all-to-all(bf16[16,104,128]{2,1,0:T(8,128)(2,1)S(1)} %get-tuple-element.11), channel_id=1, replica_groups=mesh['cfg'=2,'z'=16,'x'=4,'req'=4] {'x','req'}, dimensions={0} | all-to-all | bytes 851968 | tf_op jit(solution)/shard_map/all_to_all | solution.py:403
  45.7 0.0 copy-done.7
  45.7 0.6 shard_map.183
  46.3 19.4 %all_to_all.37.in_ref.attention_ref = bf16[16,16,128]{2,1,0:T(8,128)(2,1)S(1)} all-to-all(bf16[16,16,128]{2,1,0:T(8,128)(2,1)S(1)} %shard_map.183), channel_id=1, replica_groups=mesh['cfg'=2,'z'=16,'x'=4,'req'=4] {'z'}, dimensions={0} | all-to-all | bytes 131072 | tf_op jit(solution)/shard_map/all_to_all | solution.py:403
  65.7 10.6 %all_to_all.38.in_ref = bf16[16,16,128]{2,1,0:T(8,128)(2,1)S(1)} all-to-all(bf16[16,16,128]{2,1,0:T(8,128)(2,1)S(1)} %shard_map.184), channel_id=1, replica_groups=mesh['cfg'=2,'z'=16,'x'=4,'req'=4] {'x','req'}, dimensions={0} | all-to-all | bytes 131072 | tf_op jit(solution)/shard_map/all_to_all | solution.py:403
  76.3 0.0 copy-done.1
  76.4 0.9 shard_map.185
  77.3 9.6 %all_to_all.39.in_ref = bf16[16,16,128]{2,1,0:T(8,128)(2,1)S(1)} all-to-all(bf16[16,16,128]{2,1,0:T(8,128)(2,1)S(1)} %shard_map.185), channel_id=1, replica_groups=mesh['cfg'=2,'z'=16,'x'=4,'req'=4] {'x','req'}, dimensions={0} | all-to-all | bytes 131072 | tf_op jit(solution)/shard_map/all_to_all | solution.py:403
  86.9 14.4 %all_to_all.40.in_ref = bf16[16,16,128]{2,1,0:T(8,128)(2,1)S(1)} all-to-all(bf16[16,16,128]{2,1,0:T(8,128)(2,1)S(1)} %shard_map.186), channel_id=1, replica_groups=mesh['cfg'=2,'z'=16,'x'=4,'req'=4] {'z'}, dimensions={0} | all-to-all | bytes 131072 | tf_op jit(solution)/shard_map/all_to_all | solution.py:403
  101.4 17.8 %all_to_all.41.in_ref = bf16[32,8,128]{2,1,0:T(8,128)(2,1)S(1)} all-to-all(bf16[32,8,128]{2,1,0:T(8,128)(2,1)S(1)} %shard_map.187), channel_id=1, replica_groups=mesh['cfg'=2,'z'=16,'x'=4,'req'=4] {'cfg','x','req'}, dimensions={0} | all-to-all | bytes 131072 | tf_op jit(solution)/shard_map/all_to_all | solution.py:403
  119.2 0.9 shard_map.188
  (13 shorter events, 0.1 us)
Async XLA Ops:
  2.6 27.9 %copy-start.5 = (bf16[64,2048]{1,0:T(8,128)(2,1)S(1)}, bf16[64,2048]{1,0:T(8,128)(2,1)}, u32[]{:S(2)}) copy-start(bf16[64,2048]{1,0:T(8,128)(2,1)} %weight_ref.1) | copy-start | bytes 786436
  2.6 27.9 %copy-start.8 = (bf16[2048]{0:T(1024)(128)(2,1)S(1)}, bf16[2048]{0:T(1024)(128)(2,1)}, u32[]{:S(2)}) copy-start(bf16[2048]{0:T(1024)(128)(2,1)} %first_gain_ref.1) | copy-start | bytes 12292
  2.6 27.9 %copy-start.9 = (bf16[2048]{0:T(1024)(128)(2,1)S(1)}, bf16[2048]{0:T(1024)(128)(2,1)}, u32[]{:S(2)}) copy-start(bf16[2048]{0:T(1024)(128)(2,1)} %second_gain_ref.1) | copy-start | bytes 12292
  2.6 43.1 %copy-start.7 = (bf16[2048,8]{0,1:T(8,128)(2,1)S(1)}, bf16[2048,8]{0,1:T(8,128)(2,1)}, u32[]{:S(2)}) copy-start(bf16[2048,8]{0,1:T(8,128)(2,1)} %param.27) | copy-start | bytes 98308
  30.5 15.2 %copy-start.3 = (bf16[1,16,2048]{2,1,0:T(8,128)(2,1)S(1)}, bf16[1,16,2048]{2,1,0:T(8,128)(2,1)}, u32[]{:S(2)}) copy-start(bf16[1,16,2048]{2,1,0:T(8,128)(2,1)} %residual_ref.5) | copy-start | bytes 196612
  30.5 15.2 %copy-start.10 = (s32[16,2]{0,1:T(2,128)S(1)}, s32[16,2]{0,1:T(2,128)}, u32[]{:S(2)}) copy-start(s32[16,2]{0,1:T(2,128)} %param.25) | copy-start | bytes 388
  30.5 45.8 %copy-start.2 = (bf16[176,2048]{1,0:T(8,128)(2,1)S(1)}, bf16[176,2048]{1,0:T(8,128)(2,1)}, u32[]{:S(2)}) copy-start(bf16[176,2048]{1,0:T(8,128)(2,1)} %down_ref.1) | copy-start | bytes 2162692
  30.9 45.5 %copy-start = (bf16[176,2048]{1,0:T(8,128)(2,1)S(1)}, bf16[176,2048]{1,0:T(8,128)(2,1)}, u32[]{:S(2)}) copy-start(bf16[176,2048]{1,0:T(8,128)(2,1)} %gate_ref.1) | copy-start | bytes 2162692
  30.9 45.5 %copy-start.1 = (bf16[176,2048]{1,0:T(8,128)(2,1)S(1)}, bf16[176,2048]{1,0:T(8,128)(2,1)}, u32[]{:S(2)}) copy-start(bf16[176,2048]{1,0:T(8,128)(2,1)} %up_ref.1) | copy-start | bytes 2162692
  65.7 10.6 %copy-start.6 = (bf16[2048,8]{0,1:T(8,128)(2,1)S(1)}, bf16[2048,8]{0,1:T(8,128)(2,1)}, u32[]{:S(2)}) copy-start(bf16[2048,8]{0,1:T(8,128)(2,1)} %param.28) | copy-start | bytes 98308
  77.3 41.9 %copy-start.4 = (bf16[125,2048]{1,0:T(8,128)(2,1)S(1)}, bf16[125,2048]{1,0:T(8,128)(2,1)}, u32[]{:S(2)}) copy-start(bf16[125,2048]{1,0:T(8,128)(2,1)} %words_ref.1) | copy-start | bytes 1536004

commit v5 on v4

--- a/solution.py
+++ b/solution.py
@@ -20,6 +20,10 @@
 HEADS_ROW = 4
 ROW = HEADS_ROW * HD + LANES
 SCALE = 1.0 / math.sqrt(HD)
+
+GATE_LANE = 12
+GATE_TERMS = 3
+MERGED = HEADS_ROW * 8 + 8
 
 F32 = jnp.float32
 BF16 = jnp.bfloat16
@@ -267,12 +271,11 @@
 
 
 def merge_kernel(
-    in_ref, weight_ref, first_gain_ref, second_gain_ref, out_ref, gains_ref
+    in_ref, residual_ref, router_ref, ids_ref, first_gain_ref, second_gain_ref, out_ref, gains_ref
 ):
     gains_ref[0, :] = first_gain_ref[...].astype(F32)
     gains_ref[1, :] = second_gain_ref[...].astype(F32)
     wide = HEADS_ROW * HD
-    copies = out_ref.shape[0]
     stats = in_ref[:, :, wide:].astype(F32)[:, None]
     numerator, denominator, peak = merged(
         lambda n, g: in_ref[n, :, :wide].astype(F32), stats, 1
@@ -284,54 +287,82 @@
         high = total.astype(BF16).astype(F32)
         packed = jnp.where(lane == 4 + j, high, packed)
         packed = jnp.where(lane == 8 + j, total - high, packed)
-    blocks = [numerator[0][:, j * HD : (j + 1) * HD] for j in range(HEADS_ROW)] + [packed]
-    blocks = [block.astype(BF16) for block in blocks]
-    for copy in range(copies):
-        for j, block in enumerate(blocks):
-            out_ref[copy, j * 8 : (j + 1) * 8, :] = block
-        out_ref[copy, len(blocks) * 8 :, :] = weight_ref[:, copy * LANES : (copy + 1) * LANES]
-
-
-def project_kernel(in_ref, residual_ref, router_ref, ids_ref, out_ref, stats_ref, weight_ref):
-    requests = 4
-    columns, groups = 4, 4
-    head_rows = HEADS_ROW * 8
-    weight_rows = in_ref.shape[1] - head_rows - 8
-    sources = in_ref.shape[0]
-    expert = expert_of_plane()
-    for source in range(sources):
-        stats_ref[source] = in_ref[source, head_rows : head_rows + 8, :].astype(F32)
-        weight_ref[source * weight_rows : (source + 1) * weight_rows, :] = in_ref[
-            source, head_rows + 8 :, :
-        ]
-    stats = stats_ref[...].reshape(columns, groups, 8, LANES)
-
-    def part(n, g):
-        source = n * groups + g
-        return jnp.concatenate(
-            [in_ref[source, j * 8 : (j + 1) * 8, :] for j in range(HEADS_ROW)], axis=1
-        ).astype(F32)
-
-    numerator, denominator, _ = merged(part, stats, groups)
     inputs = residual_ref[0].astype(F32)
     normed = (inputs * rms(inputs)).astype(BF16)
     logits = lax.dot_general(router_ref[...], normed, NT, preferred_element_type=F32)
-    row = iota((8 * groups, 1), 0)
-    gate = share_column(logits, ids_ref, expert, row // 8 * requests + row % requests)
-    attended = jnp.concatenate(
-        [top / jnp.maximum(bottom, 1e-30) for top, bottom in zip(numerator, denominator)], axis=0
-    )
-    gated = (attended.astype(BF16).astype(F32) * gate).astype(BF16)
+    request = lax.axis_index("req") * 4 + iota((8, 1), 0) % 4
+    rest = share_column(logits, ids_ref, expert_of_plane(), request)
+    for term in range(GATE_TERMS):
+        piece = rest.astype(BF16).astype(F32)
+        packed = jnp.where(lane == GATE_LANE + term, piece, packed)
+        rest = rest - piece
+    chunk = lax.axis_index("x") * lax.axis_size("req") + lax.axis_index("req")
+    features = pl.ds(pl.multiple_of(chunk * LANES, LANES), LANES)
+    blocks = [numerator[0][:, j * HD : (j + 1) * HD] for j in range(HEADS_ROW)] + [packed]
+    stream = lax.axis_index("cfg")
+    for s in range(out_ref.shape[0]):
+        for j, block in enumerate(blocks):
+            at = slice(j * 8, (j + 1) * 8)
+            out_ref[s, at, :] = jnp.where(stream == s, block, 0.0).astype(BF16)
+        own = residual_ref[0, :, features].astype(F32)
+        out_ref[s, len(blocks) * 8 :, :] = jnp.where(stream == s, own, 0.0).astype(BF16)
+
+
+def pack_kernel(in_ref, weight_ref, out_ref):
+    streams = in_ref.shape[0]
+    for copy in range(out_ref.shape[0]):
+        for s in range(streams):
+            out_ref[copy, s * MERGED : (s + 1) * MERGED, :] = in_ref[s, :MERGED, :]
+        out_ref[copy, streams * MERGED :, :] = weight_ref[:, copy * LANES : (copy + 1) * LANES]
+
+
+def project_kernel(in_ref, out_ref, stats_ref, weight_ref):
+    requests = 4
+    columns, groups = 4, 4
+    streams = stats_ref.shape[0]
+    head_rows = HEADS_ROW * 8
+    weight_at = streams * MERGED
+    weight_rows = in_ref.shape[1] - weight_at
+    sources = in_ref.shape[0]
+    for source in range(sources):
+        for s in range(streams):
+            at = s * MERGED + head_rows
+            stats_ref[s, source] = in_ref[source, at : at + 8, :].astype(F32)
+        weight_ref[source * weight_rows : (source + 1) * weight_rows, :] = in_ref[
+            source, weight_at:, :
+        ]
+    gated = []
+    for s in range(streams):
+        stats = stats_ref[s].reshape(columns, groups, 8, LANES)
+
+        def part(n, g, base=s * MERGED):
+            source = n * groups + g
+            return jnp.concatenate(
+                [in_ref[source, base + j * 8 : base + (j + 1) * 8, :] for j in range(HEADS_ROW)],
+                axis=1,
+            ).astype(F32)
+
+        numerator, denominator, _ = merged(part, stats, groups)
+        terms = stats_ref[s, :groups].reshape(8 * groups, LANES)
+        lane = iota(terms.shape, 1)
+        is_gate = (lane >= GATE_LANE) & (lane < GATE_LANE + GATE_TERMS)
+        gate = jnp.sum(jnp.where(is_gate, terms, 0.0), axis=1, keepdims=True)
+        attended = jnp.concatenate(
+            [top / jnp.maximum(bottom, 1e-30) for top, bottom in zip(numerator, denominator)],
+            axis=0,
+        )
+        gated.append((attended.astype(BF16).astype(F32) * gate).astype(BF16))
+    gated = jnp.concatenate(gated, axis=0)
     wide = HEADS_ROW * HD
     lower = dot(gated, weight_ref[:wide, :])
     upper = dot(gated, weight_ref[wide:, :])
-    mixed = jnp.where(row % 8 < requests, lower, upper)
+    mixed = jnp.where(iota((8 * groups * streams, 1), 0) % 8 < requests, lower, upper)
     sub = iota((8, LANES), 0)
     tiles = []
-    for g in range(groups):
+    for g in range(groups * streams):
         tile = mixed[g * 8 : (g + 1) * 8]
         tiles.append(tile + pltpu.roll(tile, 4, 0))
-    for pair in range(groups // 2):
+    for pair in range(groups * streams // 2):
         both = jnp.where(sub < requests, tiles[2 * pair], tiles[2 * pair + 1]).astype(BF16)
         for copy in range(out_ref.shape[0]):
             out_ref[copy, pair * 8 : (pair + 1) * 8, :] = both
@@ -346,18 +377,37 @@
         out_ref[copy] = total
 
 
+def middle_kernel(in_ref, own_ref, out_ref):
+    total = in_ref[0].astype(F32)
+    for n in range(1, in_ref.shape[0]):
+        total = total + in_ref[n].astype(F32)
+    requests = total.shape[0] // own_ref.shape[0]
+    for s in range(own_ref.shape[0]):
+        rows = slice(s * requests, (s + 1) * requests)
+        middle = (total[rows] + own_ref[s, MERGED:, :].astype(F32)).astype(BF16)
+        for copy in range(out_ref.shape[0]):
+            out_ref[copy, rows, :] = middle
+
+
 def expert_kernel(
-    in_ref, residual_ref, gain_ref, router_ref, ids_ref, gate_ref, up_ref, down_ref, out_ref, middle_ref
+    in_ref, gain_ref, router_ref, ids_ref, gate_ref, up_ref, down_ref, out_ref, middle_ref
 ):
     chunks = in_ref.shape[0]
-    requests = in_ref.shape[1]
+    requests = ids_ref.shape[1]
+    streams = in_ref.shape[1] // requests
     for chunk in range(chunks):
         at = slice(chunk * LANES, (chunk + 1) * LANES)
-        middle_ref[:, at] = residual_ref[0, :, at].astype(F32) + in_ref[chunk].astype(F32)
+        middle_ref[:, at] = in_ref[chunk].astype(F32)
     middle = middle_ref[...]
     inputs = (middle * rms(middle) * gain_ref[0:1, :]).astype(BF16)
-    logits = lax.dot_general(router_ref[...], inputs, NT, preferred_element_type=F32)
-    share = share_column(logits, ids_ref, expert_of_plane(), iota((requests, 1), 0))
+    shares = []
+    for s in range(streams):
+        rows = slice(s * requests, (s + 1) * requests)
+        logits = lax.dot_general(router_ref[...], inputs[rows], NT, preferred_element_type=F32)
+        shares.append(
+            share_column(logits, ids_ref, expert_of_plane(), iota((requests, 1), 0))
+        )
+    share = jnp.concatenate(shares, axis=0)
     gate = lax.dot_general(inputs, gate_ref[...], NT, preferred_element_type=F32)
     up = lax.dot_general(inputs, up_ref[...], NT, preferred_element_type=F32)
     hidden = (gate / (1.0 + jnp.exp(-gate)) * up * share).astype(BF16)
@@ -366,31 +416,32 @@
         out_ref[chunk] = dot(hidden, down_ref[:, at]).astype(BF16)
 
 
-def finish_kernel(in_ref, attention_ref, residual_ref, out_ref):
+def finish_kernel(in_ref, attention_ref, own_ref, out_ref):
     total = attention_ref[0].astype(F32)
     for n in range(1, attention_ref.shape[0]):
         total = total + attention_ref[n].astype(F32)
     for n in range(in_ref.shape[0]):
         total = total + in_ref[n].astype(F32)
-    chunk = lax.axis_index("x") * lax.axis_size("req") + lax.axis_index("req")
-    at = pl.ds(pl.multiple_of(chunk * LANES, LANES), LANES)
-    total = (total + residual_ref[0, :, at].astype(F32)).astype(out_ref.dtype)
-    half = out_ref.shape[1]
+    streams = own_ref.shape[0]
+    requests = total.shape[0] // streams
+    half = requests // 2
     copies = out_ref.shape[0] // 2
-    for stream in range(2):
-        for copy in range(copies):
-            out_ref[stream * copies + copy] = total[stream * half : (stream + 1) * half]
+    for s in range(streams):
+        rows = total[s * requests : (s + 1) * requests] + own_ref[s, MERGED:, :].astype(F32)
+        rows = rows.astype(out_ref.dtype)
+        for core in range(2):
+            for copy in range(copies):
+                out_ref[core * copies + copy, s * half : (s + 1) * half, :] = rows[
+                    core * half : (core + 1) * half
+                ]
 
 
 def head_kernel(in_ref, gain_ref, words_ref, factor_ref, out_ref, joined_ref):
-    half = in_ref.shape[1]
     chunks = in_ref.shape[0] // 2
-    for stream in range(2):
-        for chunk in range(chunks):
-            at = slice(chunk * LANES, (chunk + 1) * LANES)
-            joined_ref[stream * half : (stream + 1) * half, at] = in_ref[
-                stream * chunks + chunk
-            ].astype(F32)
+    half = out_ref.shape[0]
+    for chunk in range(chunks):
+        at = slice(chunk * LANES, (chunk + 1) * LANES)
+        joined_ref[:, at] = in_ref[chunks + chunk].astype(F32)
     joined = joined_ref[...]
     inputs = (joined * rms(joined) * gain_ref[1:2, :]).astype(BF16)
     logits = lax.dot_general(inputs, words_ref[...], NT, preferred_element_type=F32)
@@ -424,7 +475,7 @@
     tenant_sizes,
     guidance,
 ):
-    planes = lax.axis_size("z")
+    planes, streams = lax.axis_size("z"), lax.axis_size("cfg")
     plane = ("x", "req")
     members = lax.axis_size(plane)
     requests = residual.shape[1]
@@ -470,51 +521,54 @@
         )
     )
     partial = exchanged(partial, "z")
-
-    weight_rows = attention_output.shape[0]
-    merged_rows = HEADS_ROW * 8 + 8 + weight_rows
-    both, gains = call(
+    own, gains = call(
         merge_kernel,
-        (shape((members, merged_rows, LANES), BF16), shape((2, D), F32)),
-        [vmem()] * 4,
-    )(partial, attention_output, expert_gain, final_gain)
-    both = exchanged(both, plane)
-
-    chunk = shape((planes, requests, LANES), BF16)
-    projected = call(
-        project_kernel,
-        chunk,
-        [vmem()] * 4,
-        [pltpu.VMEM((members, 8, LANES), F32), pltpu.VMEM((members * weight_rows, LANES), BF16)],
-    )(both, residual, attention_router.T, attention_ids.T)
-    projected = exchanged(projected, "z")
-
-    spread = shape((members, requests, LANES), BF16)
-    attention = call(fold_kernel, spread, [vmem()])(projected)
-    attention = exchanged(attention, plane)
-
-    hidden = call(
-        expert_kernel, spread, [vmem()] * 8, [pltpu.VMEM((requests, D), F32)]
-    )(
-        attention,
-        residual,
-        gains,
-        expert_router.T,
-        ids,
-        expert_gate,
-        expert_up,
-        expert_down,
-    )
-    hidden = exchanged(hidden, plane)
-    hidden = call(fold_kernel, chunk, [vmem()])(hidden)
-    hidden = exchanged(hidden, "z")
-
-    streams = lax.axis_size("cfg")
-    final = call(
-        finish_kernel, shape((streams * members, requests // 2, LANES), BF16), [vmem()] * 3
-    )(hidden, projected, residual)
+        (shape((streams, MERGED + requests, LANES), BF16), shape((2, D), F32)),
+        [vmem()] * 6,
+    )(partial, residual, attention_router.T, attention_ids.T, expert_gain, final_gain)
+    own = lax.psum(own, "cfg")
+
+    def middle(own):
+        weight_rows = attention_output.shape[0]
+        packed = call(
+            pack_kernel,
+            shape((members, streams * MERGED + weight_rows, LANES), BF16),
+            [vmem()] * 2,
+        )(own, attention_output)
+        packed = exchanged(packed, plane)
+
+        chunk = shape((planes, streams * requests, LANES), BF16)
+        projected = call(
+            project_kernel,
+            chunk,
+            [vmem()],
+            [
+                pltpu.VMEM((streams, members, 8, LANES), F32),
+                pltpu.VMEM((members * weight_rows, LANES), BF16),
+            ],
+        )(packed)
+        projected = exchanged(projected, "z")
+
+        spread = shape((members, streams * requests, LANES), BF16)
+        attention = call(middle_kernel, spread, [vmem()] * 2)(projected, own)
+        attention = exchanged(attention, plane)
+        hidden = call(
+            expert_kernel, spread, [vmem()] * 7, [pltpu.VMEM((streams * requests, D), F32)]
+        )(attention, gains, expert_router.T, ids, expert_gate, expert_up, expert_down)
+        hidden = exchanged(hidden, plane)
+        hidden = call(fold_kernel, chunk, [vmem()])(hidden)
+        hidden = exchanged(hidden, "z")
+        return call(
+            finish_kernel, shape((2 * members, requests, LANES), BF16), [vmem()] * 3
+        )(hidden, projected, own)
+
+    final = lax.cond(
+        lax.axis_index("cfg") == 1,
+        middle,
+        lambda own: jnp.zeros((2 * members, requests, LANES), BF16),
+        own,
+    )
     final = exchanged(final, ("cfg",) + plane)
-
     return call(
         head_kernel,
         shape((requests // 2, unembedding.shape[0]), F32),

time: 121 us -> 121 us (level)
  blocking collectives: 115 us -> 85.6 us
  starting transfers between devices: 0 us -> 15.9 us
  waiting for transfers between devices: 0 us -> 12.2 us
    all_to_all x7 -> x6, blocking collectives: 115 us -> 77.9 us  [exchanged(): return lax.all_to_all(value, axis, 0, 0, tiled=True)]
    all_to_all x0 -> x1, starting transfers between devices: none -> 15.9 us  [exchanged(): return lax.all_to_all(value, axis, 0, 0, tiled=True)]
    all_to_all x0 -> x1, waiting for transfers between devices: none -> 12.2 us  [exchanged(): return lax.all_to_all(value, axis, 0, 0, tiled=True)]
    psum x0 -> x1, blocking collectives: none -> 7.72 us  [local(): own = lax.psum(own, 'cfg')]
  transfers between devices with their start and end apart: 0 -> 1, of which waited for: 0 -> 1; matrix products, arithmetic and copies ran while one was open for 0% -> 0% of each run, Pallas kernels for 0% -> 0%
where the time goes in v5:
time: 121 us; the launch traced here: 120 us
  blocking collectives  85.6 us (71%)
  starting transfers between devices  15.9 us (13%)
  waiting for transfers between devices  12.2 us (10%)
  Pallas kernels  6.49 us (5%)
    all_to_all x6, blocking collectives, exchanged(): return lax.all_to_all(value, axis, 0, 0, tiled=True)  77.9 us
    all_to_all x1, starting transfers between devices, exchanged(): return lax.all_to_all(value, axis, 0, 0, tiled=True)  15.9 us
    all_to_all x1, waiting for transfers between devices, exchanged(): return lax.all_to_all(value, axis, 0, 0, tiled=True)  12.2 us
    psum x1, blocking collectives, local(): own = lax.psum(own, 'cfg')  7.72 us
    pallas_call x1, Pallas kernels, local(): call(attend_kernel, (shape((planes, 8, ROW), BF16), shape((requests // 2,...  3.34 us
  transfers between devices with their start and end apart: 1, of which 1 were waited for; matrix products, arithmetic and copies ran while one was open for 0% of the time, Pallas kernels for 0%

profile of v5, /device:TPU:1, one launch (start us, length us, event | category | flops | bytes accessed | tf_op | source)
XLA Modules:
  0.0 120.4 jit_solution(15255510155198411601)
XLA Ops:
  0.0 3.3 %shard_map.186 = (bf16[16,8,640]{2,1,0:T(8,128)(2,1)}, f32[8,128]{1,0:T(8,128)S(1)}, s32[2,16]{1,0:T(2,128)S(1)}) custom-call(bf16[1,4,4096]{2,1,0:T(4,128)(2,1)} %q_hbm.1, bf16[1,4,48,2048]{3,2,1,0:T(8,128)(2,1)} %k_hbm.1, bf16[1,4,48,2048]{3,2,1,0:T(8,128)(2,1)} %v_hbm.1, bf16[1,4,2,2048]{3,2,1,0:T(2,128)(2,1)} %new_hbm.1, s32[1,4]{1,0:T(1,128)} %lengths_hbm.1, ...), custom_call_target="tpu_custom_call" | custom-call | tf_op jit(solution)/shard_map/pallas_call | solution.py:485
  3.4 0.0 copy-start.1
  3.4 0.0 copy-start.2
  3.4 15.9 %all-to-all-start.5 = ((bf16[16,8,640]{2,1,0:T(8,128)(2,1)}), bf16[16,8,640]{2,1,0:T(8,128)(2,1)S(1)}, u32[]{:S(2)}, u32[]{:S(2)}) async-start(bf16[16,8,640]{2,1,0:T(8,128)(2,1)} %get-tuple-element.37), calls=%async_computation.5 | async-start | bytes 327680 | tf_op jit(solution)/shard_map/all_to_all | solution.py:454
  19.3 0.0 copy-start.4
  19.3 0.0 copy-start.3
  19.3 0.0 copy-start.5
  19.3 12.2 %all-to-all-done.5.in_ref = bf16[16,8,640]{2,1,0:T(8,128)(2,1)S(1)} async-done(((bf16[16,8,640]{2,1,0:T(8,128)(2,1)}), bf16[16,8,640]{2,1,0:T(8,128)(2,1)S(1)}, u32[]{:S(2)}, u32[]{:S(2)}) %all-to-all-start.5) | async-done | bytes 163872 | tf_op jit(solution)/shard_map/all_to_all | solution.py:454
  31.5 0.0 copy-done.1
  31.5 0.4 shard_map.187
  32.0 7.7 %psum.7 = bf16[2,56,128]{2,1,0:T(8,128)(2,1)S(1)} all-reduce(bf16[2,56,128]{2,1,0:T(8,128)(2,1)S(1)} %get-tuple-element.38), channel_id=1, replica_groups=mesh['cfg'=2,'z'=16,'x'=4,'req'=4] {'cfg'}, use_global_device_ids=true, to_apply=%region_0.0 | all-reduce | flops 14336 | bytes 57344 | tf_op jit(solution)/shard_map/psum | solution.py:529
  39.7 0.0 copy-start
  39.7 68.6 %conditional.1 = (bf16[32,16,128]{2,1,0:T(8,128)(2,1)S(1)}) conditional(s32[]{:T(128)} %convert_element_type.3, () %tuple.11, (bf16[2,56,128]{2,1,0:T(8,128)(2,1)S(1)}, bf16[64,2048]{1,0:T(8,128)(2,1)S(1)}, bf16[2048,8]{0,1:T(8,128)(2,1)S(1)}, f32[2,2048]{1,0:T(2,128)S(1)}, s32[2,16]{1,0:T(2,128)S(1)}, /*index=5*/bf16[176,2048]{1,0:T(8,128)(2,1)S(1)}, ...), branch_computations={%region_1.0_spmd, %region_2.0_spmd} | conditional | bytes 5111844 | solution.py:565
  39.8 0.1 branch_1_fun.6
  39.9 16.0 %all_to_all.30.in_ref = bf16[16,144,128]{2,1,0:T(8,128)(2,1)S(1)} all-to-all(bf16[16,144,128]{2,1,0:T(8,128)(2,1)S(1)} %branch_1_fun.6), channel_id=1, replica_groups=mesh['cfg'=2,'z'=16,'x'=4,'req'=4] {'x','req'}, dimensions={0} | all-to-all | bytes 1179648 | tf_op jit(solution)/shard_map/cond/branch_1_fun/all_to_all | solution.py:454
  55.9 0.5 branch_1_fun.7
  56.4 15.8 %all_to_all.31.in_ref.attention_ref = bf16[16,32,128]{2,1,0:T(8,128)(2,1)S(1)} all-to-all(bf16[16,32,128]{2,1,0:T(8,128)(2,1)S(1)} %branch_1_fun.7), channel_id=1, replica_groups=mesh['cfg'=2,'z'=16,'x'=4,'req'=4] {'z'}, dimensions={0} | all-to-all | bytes 262144 | tf_op jit(solution)/shard_map/cond/branch_1_fun/all_to_all | solution.py:454
  72.2 9.6 %all_to_all.32.in_ref = bf16[16,32,128]{2,1,0:T(8,128)(2,1)S(1)} all-to-all(bf16[16,32,128]{2,1,0:T(8,128)(2,1)S(1)} %branch_1_fun.8), channel_id=1, replica_groups=mesh['cfg'=2,'z'=16,'x'=4,'req'=4] {'x','req'}, dimensions={0} | all-to-all | bytes 262144 | tf_op jit(solution)/shard_map/cond/branch_1_fun/all_to_all | solution.py:454
  81.9 1.1 branch_1_fun.9
  83.0 9.8 %all_to_all.33.in_ref = bf16[16,32,128]{2,1,0:T(8,128)(2,1)S(1)} all-to-all(bf16[16,32,128]{2,1,0:T(8,128)(2,1)S(1)} %branch_1_fun.9), channel_id=1, replica_groups=mesh['cfg'=2,'z'=16,'x'=4,'req'=4] {'x','req'}, dimensions={0} | all-to-all | bytes 262144 | tf_op jit(solution)/shard_map/cond/branch_1_fun/all_to_all | solution.py:454
  92.8 15.5 %all_to_all.34.in_ref = bf16[16,32,128]{2,1,0:T(8,128)(2,1)S(1)} all-to-all(bf16[16,32,128]{2,1,0:T(8,128)(2,1)S(1)} %branch_1_fun.10), channel_id=1, replica_groups=mesh['cfg'=2,'z'=16,'x'=4,'req'=4] {'z'}, dimensions={0} | all-to-all | bytes 262144 | tf_op jit(solution)/shard_map/cond/branch_1_fun/all_to_all | solution.py:454
  108.3 0.1 branch_1_fun.11
  108.4 11.1 %all_to_all.35.in_ref = bf16[32,16,128]{2,1,0:T(8,128)(2,1)S(1)} all-to-all(bf16[32,16,128]{2,1,0:T(8,128)(2,1)S(1)} %get-tuple-element.52), channel_id=1, replica_groups=mesh['cfg'=2,'z'=16,'x'=4,'req'=4] {'cfg','x','req'}, dimensions={0} | all-to-all | bytes 262144 | tf_op jit(solution)/shard_map/all_to_all | solution.py:454
  119.5 0.9 shard_map.188
  (17 shorter events, 0.1 us)
Async XLA Ops:
  0.0 39.7 %copy-start.6 = (bf16[176,2048]{1,0:T(8,128)(2,1)S(1)}, bf16[176,2048]{1,0:T(8,128)(2,1)}, u32[]{:S(2)}) copy-start(bf16[176,2048]{1,0:T(8,128)(2,1)} %param.33) | copy-start | bytes 2162692
  0.0 39.7 %copy-start.7 = (bf16[176,2048]{1,0:T(8,128)(2,1)S(1)}, bf16[176,2048]{1,0:T(8,128)(2,1)}, u32[]{:S(2)}) copy-start(bf16[176,2048]{1,0:T(8,128)(2,1)} %param.34) | copy-start | bytes 2162692
  0.0 39.7 %copy-start.9 = (bf16[64,2048]{1,0:T(8,128)(2,1)S(1)}, bf16[64,2048]{1,0:T(8,128)(2,1)}, u32[]{:S(2)}) copy-start(bf16[64,2048]{1,0:T(8,128)(2,1)} %param.31) | copy-start | bytes 786436
  3.4 28.1 %copy-start.1 = (bf16[1,16,2048]{2,1,0:T(8,128)(2,1)S(1)}, bf16[1,16,2048]{2,1,0:T(8,128)(2,1)}, u32[]{:S(2)}) copy-start(bf16[1,16,2048]{2,1,0:T(8,128)(2,1)} %residual_ref.1) | copy-start | bytes 196612
  3.4 28.1 %copy-start.2 = (bf16[2048,8]{0,1:T(8,128)(2,1)S(1)}, bf16[2048,8]{0,1:T(8,128)(2,1)}, u32[]{:S(2)}) copy-start(bf16[2048,8]{0,1:T(8,128)(2,1)} %param.29) | copy-start | bytes 98308
  3.4 28.1 %all-to-all-start.5 = ((bf16[16,8,640]{2,1,0:T(8,128)(2,1)}), bf16[16,8,640]{2,1,0:T(8,128)(2,1)S(1)}, u32[]{:S(2)}, u32[]{:S(2)}) async-start(bf16[16,8,640]{2,1,0:T(8,128)(2,1)} %get-tuple-element.37), calls=%async_computation.5 | async-start | bytes 327680 | tf_op jit(solution)/shard_map/all_to_all | solution.py:454
  19.3 12.2 %copy-start.4 = (bf16[2048]{0:T(1024)(128)(2,1)S(1)}, bf16[2048]{0:T(1024)(128)(2,1)}, u32[]{:S(2)}) copy-start(bf16[2048]{0:T(1024)(128)(2,1)} %second_gain_ref.1) | copy-start | bytes 12292
  19.3 12.2 %copy-start.3 = (bf16[2048]{0:T(1024)(128)(2,1)S(1)}, bf16[2048]{0:T(1024)(128)(2,1)}, u32[]{:S(2)}) copy-start(bf16[2048]{0:T(1024)(128)(2,1)} %first_gain_ref.1) | copy-start | bytes 12292
  19.3 12.2 %copy-start.5 = (s32[16,2]{0,1:T(2,128)S(1)}, s32[16,2]{0,1:T(2,128)}, u32[]{:S(2)}) copy-start(s32[16,2]{0,1:T(2,128)} %param.27) | copy-start | bytes 388
  32.0 7.8 %copy-start.10 = (bf16[2048,8]{0,1:T(8,128)(2,1)S(1)}, bf16[2048,8]{0,1:T(8,128)(2,1)}, u32[]{:S(2)}) copy-start(bf16[2048,8]{0,1:T(8,128)(2,1)} %param.30) | copy-start | bytes 98308
  39.7 79.8 %copy-start = (bf16[125,2048]{1,0:T(8,128)(2,1)S(1)}, bf16[125,2048]{1,0:T(8,128)(2,1)}, u32[]{:S(2)}) copy-start(bf16[125,2048]{1,0:T(8,128)(2,1)} %words_ref.1) | copy-start | bytes 1536004
  55.9 26.0 %copy-start.8 = (bf16[176,2048]{1,0:T(8,128)(2,1)S(1)}, bf16[176,2048]{1,0:T(8,128)(2,1)}, u32[]{:S(2)}) copy-start(bf16[176,2048]{1,0:T(8,128)(2,1)} %get-tuple-element.51.down_ref) | copy-start | bytes 2162692 | tf_op jit(solution)/shard_map/cond

commit v6 on v4

--- a/solution.py
+++ b/solution.py
@@ -112,8 +112,7 @@
     guidance_ref,
     rows_ref,
     small_sems,
-    key_sems,
-    value_sems,
+    cache_sems,
 ):
     requests, positions = k_hbm.shape[1], k_hbm.shape[2]
     small = [
@@ -130,26 +129,18 @@
             ]
         )
     ]
-    keys = [
-        pltpu.make_async_copy(k_hbm.at[0, r], k_ref.at[r, :positions], key_sems.at[r])
-        for r in range(requests)
-    ]
-    values_in = [
-        pltpu.make_async_copy(v_hbm.at[0, r], v_ref.at[r, :positions], value_sems.at[r])
-        for r in range(requests)
-    ]
-    small[0].start()
-    for key in keys:
-        key.start()
-    for copy in small[1:]:
+    keys = pltpu.make_async_copy(k_hbm.at[0], k_ref.at[:, :positions], cache_sems.at[0])
+    values_in = pltpu.make_async_copy(v_hbm.at[0], v_ref.at[:, :positions], cache_sems.at[1])
+    keys.start()
+    values_in.start()
+    for copy in small:
         copy.start()
-    for value in values_in:
-        value.start()
     block = lax.axis_index("z") * lax.axis_size("x") + lax.axis_index("x")
     owner = block == 0
     first_request = lax.axis_index("req") * requests
     own_head = iota((H, D), 0) == iota((H, D), 1) // HD
-    small[0].wait()
+    for copy in [*small, keys, values_in]:
+        copy.wait()
     queries = q_ref[0].astype(F32)
     wide = [
         jnp.concatenate(
@@ -161,8 +152,6 @@
         ).astype(BF16)
         for r in range(requests)
     ]
-    for copy in small[1:]:
-        copy.wait()
     new_row = (iota((SPARE, D), 0) == 0) & owner
     for r in range(requests):
         entry = new_ref[0, r].astype(F32)
@@ -171,8 +160,6 @@
     factor_ref[...] = jnp.broadcast_to(
         guidance_factor(sizes_ref, guidance_ref, factor_ref.shape[0]), factor_ref.shape
     )
-    for key in keys:
-        key.wait()
     scores = jnp.concatenate(
         [
             lax.dot_general(wide[r], k_ref[r], NT, preferred_element_type=F32)
@@ -196,8 +183,6 @@
     highs = totals.astype(BF16).astype(F32)
     lows = totals - highs
     weights = weights.astype(BF16)
-    for value in values_in:
-        value.wait()
     products = [dot(weights[r * heads : (r + 1) * heads], v_ref[r]) for r in range(requests)]
     sub = iota((8, LANES), 0)
     lane = iota((8, LANES), 1)
@@ -347,23 +332,27 @@
 
 
 def expert_kernel(
-    in_ref, residual_ref, gain_ref, router_ref, ids_ref, gate_ref, up_ref, down_ref, out_ref, middle_ref
+    in_ref, residual_ref, gain_ref, router_ref, ids_ref, gate_ref, up_ref, down_ref, out_ref
 ):
     chunks = in_ref.shape[0]
     requests = in_ref.shape[1]
-    for chunk in range(chunks):
-        at = slice(chunk * LANES, (chunk + 1) * LANES)
-        middle_ref[:, at] = residual_ref[0, :, at].astype(F32) + in_ref[chunk].astype(F32)
-    middle = middle_ref[...]
+    middle = jnp.concatenate(
+        [
+            residual_ref[0, :, chunk * LANES : (chunk + 1) * LANES].astype(F32)
+            + in_ref[chunk].astype(F32)
+            for chunk in range(chunks)
+        ],
+        axis=1,
+    )
     inputs = (middle * rms(middle) * gain_ref[0:1, :]).astype(BF16)
     logits = lax.dot_general(router_ref[...], inputs, NT, preferred_element_type=F32)
     share = share_column(logits, ids_ref, expert_of_plane(), iota((requests, 1), 0))
     gate = lax.dot_general(inputs, gate_ref[...], NT, preferred_element_type=F32)
     up = lax.dot_general(inputs, up_ref[...], NT, preferred_element_type=F32)
     hidden = (gate / (1.0 + jnp.exp(-gate)) * up * share).astype(BF16)
+    out = dot(hidden, down_ref[...])
     for chunk in range(chunks):
-        at = slice(chunk * LANES, (chunk + 1) * LANES)
-        out_ref[chunk] = dot(hidden, down_ref[:, at]).astype(BF16)
+        out_ref[chunk] = out[:, chunk * LANES : (chunk + 1) * LANES].astype(BF16)
 
 
 def finish_kernel(in_ref, attention_ref, residual_ref, out_ref):
@@ -382,18 +371,21 @@
             out_ref[stream * copies + copy] = total[stream * half : (stream + 1) * half]
 
 
-def head_kernel(in_ref, gain_ref, words_ref, factor_ref, out_ref, joined_ref):
+def head_kernel(in_ref, gain_ref, words_ref, factor_ref, out_ref):
     half = in_ref.shape[1]
     chunks = in_ref.shape[0] // 2
-    for stream in range(2):
-        for chunk in range(chunks):
-            at = slice(chunk * LANES, (chunk + 1) * LANES)
-            joined_ref[stream * half : (stream + 1) * half, at] = in_ref[
-                stream * chunks + chunk
-            ].astype(F32)
-    joined = joined_ref[...]
-    inputs = (joined * rms(joined) * gain_ref[1:2, :]).astype(BF16)
+    joined = jnp.concatenate(
+        [
+            jnp.concatenate(
+                [in_ref[stream * chunks + chunk].astype(F32) for chunk in range(chunks)], axis=1
+            )
+            for stream in range(2)
+        ],
+        axis=0,
+    )
+    inputs = (joined * gain_ref[1:2, :]).astype(BF16)
     logits = lax.dot_general(inputs, words_ref[...], NT, preferred_element_type=F32)
+    logits = logits * rms(joined)
     factor = factor_ref[:, :1]
     conditional, unconditional = logits[:half], logits[half:]
     out_ref[...] = unconditional + factor * (conditional - unconditional)
@@ -450,8 +442,7 @@
             pltpu.SMEM(guidance.shape, jnp.int32),
             pltpu.VMEM((2, TOPK, 8, ROW), F32),
             pltpu.SemaphoreType.DMA((7,)),
-            pltpu.SemaphoreType.DMA((rows,)),
-            pltpu.SemaphoreType.DMA((rows,)),
+            pltpu.SemaphoreType.DMA((2,)),
         ],
     )(
         *(
@@ -493,9 +484,7 @@
     attention = call(fold_kernel, spread, [vmem()])(projected)
     attention = exchanged(attention, plane)
 
-    hidden = call(
-        expert_kernel, spread, [vmem()] * 8, [pltpu.VMEM((requests, D), F32)]
-    )(
+    hidden = call(expert_kernel, spread, [vmem()] * 8)(
         attention,
         residual,
         gains,
@@ -519,7 +508,6 @@
         head_kernel,
         shape((requests // 2, unembedding.shape[0]), F32),
         [vmem()] * 4,
-        [pltpu.VMEM((requests, D), F32)],
     )(final, gains, unembedding, factor)
 
 

time: 121 us -> 120 us (level)
  no operation moved by 1% of the time
where the time goes in v6:
time: 120 us
  blocking collectives  115 us (96%)
  Pallas kernels  5.02 us (4%)
    all_to_all x7, blocking collectives, exchanged(): return lax.all_to_all(value, axis, 0, 0, tiled=True)  115 us

profile of v6, /device:TPU:1, one launch (start us, length us, event | category | flops | bytes accessed | tf_op | source)
XLA Modules:
  0.0 119.7 jit_solution(13517492897301530890)
XLA Ops:
  0.0 2.3 %shard_map.181 = (bf16[16,8,640]{2,1,0:T(8,128)(2,1)S(1)}, f32[8,128]{1,0:T(8,128)S(1)}, s32[2,16]{1,0:T(2,128)S(1)}) custom-call(bf16[1,4,4096]{2,1,0:T(4,128)(2,1)} %q_hbm.1, bf16[1,4,48,2048]{3,2,1,0:T(8,128)(2,1)} %k_hbm.1, bf16[1,4,48,2048]{3,2,1,0:T(8,128)(2,1)} %v_hbm.1, bf16[1,4,2,2048]{3,2,1,0:T(2,128)(2,1)} %new_hbm.1, s32[1,4]{1,0:T(1,128)} %lengths_hbm.1, ...), custom_call_target="tpu_custom_call" | custom-call | tf_op jit(solution)/shard_map/pallas_call | solution.py:426
  2.4 0.0 copy-start.5
  2.4 0.0 copy-start.8
  2.4 0.0 copy-start.9
  2.4 0.0 copy-start.7
  2.4 27.9 %all_to_all.35.in_ref = bf16[16,8,640]{2,1,0:T(8,128)(2,1)S(1)} all-to-all(bf16[16,8,640]{2,1,0:T(8,128)(2,1)S(1)} %get-tuple-element.10), channel_id=1, replica_groups=mesh['cfg'=2,'z'=16,'x'=4,'req'=4] {'z'}, dimensions={0} | all-to-all | bytes 327680 | tf_op jit(solution)/shard_map/all_to_all | solution.py:395
  30.3 0.0 copy-done.9
  30.3 0.0 copy-start.3
  30.3 0.0 copy-start.10
  30.3 0.0 copy-start.2
  30.4 0.3 shard_map.182
  30.7 0.0 copy-start
  30.7 0.0 copy-start.1
  30.7 14.8 %all_to_all.36.in_ref = bf16[16,104,128]{2,1,0:T(8,128)(2,1)S(1)} all-to-all(bf16[16,104,128]{2,1,0:T(8,128)(2,1)S(1)} %get-tuple-element.11), channel_id=1, replica_groups=mesh['cfg'=2,'z'=16,'x'=4,'req'=4] {'x','req'}, dimensions={0} | all-to-all | bytes 851968 | tf_op jit(solution)/shard_map/all_to_all | solution.py:395
  45.5 0.6 shard_map.183
  46.1 19.4 %all_to_all.37.in_ref.attention_ref = bf16[16,16,128]{2,1,0:T(8,128)(2,1)S(1)} all-to-all(bf16[16,16,128]{2,1,0:T(8,128)(2,1)S(1)} %shard_map.183), channel_id=1, replica_groups=mesh['cfg'=2,'z'=16,'x'=4,'req'=4] {'z'}, dimensions={0} | all-to-all | bytes 131072 | tf_op jit(solution)/shard_map/all_to_all | solution.py:395
  65.5 10.6 %all_to_all.38.in_ref = bf16[16,16,128]{2,1,0:T(8,128)(2,1)S(1)} all-to-all(bf16[16,16,128]{2,1,0:T(8,128)(2,1)S(1)} %shard_map.184), channel_id=1, replica_groups=mesh['cfg'=2,'z'=16,'x'=4,'req'=4] {'x','req'}, dimensions={0} | all-to-all | bytes 131072 | tf_op jit(solution)/shard_map/all_to_all | solution.py:395
  76.1 0.0 copy-done.1
  76.1 0.0 copy-done.6
  76.1 0.8 shard_map.185
  77.0 9.6 %all_to_all.39.in_ref = bf16[16,16,128]{2,1,0:T(8,128)(2,1)S(1)} all-to-all(bf16[16,16,128]{2,1,0:T(8,128)(2,1)S(1)} %shard_map.185), channel_id=1, replica_groups=mesh['cfg'=2,'z'=16,'x'=4,'req'=4] {'x','req'}, dimensions={0} | all-to-all | bytes 131072 | tf_op jit(solution)/shard_map/all_to_all | solution.py:395
  86.6 14.4 %all_to_all.40.in_ref = bf16[16,16,128]{2,1,0:T(8,128)(2,1)S(1)} all-to-all(bf16[16,16,128]{2,1,0:T(8,128)(2,1)S(1)} %shard_map.186), channel_id=1, replica_groups=mesh['cfg'=2,'z'=16,'x'=4,'req'=4] {'z'}, dimensions={0} | all-to-all | bytes 131072 | tf_op jit(solution)/shard_map/all_to_all | solution.py:395
  101.1 17.8 %all_to_all.41.in_ref = bf16[32,8,128]{2,1,0:T(8,128)(2,1)S(1)} all-to-all(bf16[32,8,128]{2,1,0:T(8,128)(2,1)S(1)} %shard_map.187), channel_id=1, replica_groups=mesh['cfg'=2,'z'=16,'x'=4,'req'=4] {'cfg','x','req'}, dimensions={0} | all-to-all | bytes 131072 | tf_op jit(solution)/shard_map/all_to_all | solution.py:395
  118.9 0.9 shard_map.188
  (13 shorter events, 0.1 us)
Async XLA Ops:
  2.4 28.0 %copy-start.5 = (bf16[64,2048]{1,0:T(8,128)(2,1)S(1)}, bf16[64,2048]{1,0:T(8,128)(2,1)}, u32[]{:S(2)}) copy-start(bf16[64,2048]{1,0:T(8,128)(2,1)} %weight_ref.1) | copy-start | bytes 786436
  2.4 27.9 %copy-start.8 = (bf16[2048]{0:T(1024)(128)(2,1)S(1)}, bf16[2048]{0:T(1024)(128)(2,1)}, u32[]{:S(2)}) copy-start(bf16[2048]{0:T(1024)(128)(2,1)} %first_gain_ref.1) | copy-start | bytes 12292
  2.4 27.9 %copy-start.9 = (bf16[2048]{0:T(1024)(128)(2,1)S(1)}, bf16[2048]{0:T(1024)(128)(2,1)}, u32[]{:S(2)}) copy-start(bf16[2048]{0:T(1024)(128)(2,1)} %second_gain_ref.1) | copy-start | bytes 12292
  2.4 43.1 %copy-start.7 = (bf16[2048,8]{0,1:T(8,128)(2,1)S(1)}, bf16[2048,8]{0,1:T(8,128)(2,1)}, u32[]{:S(2)}) copy-start(bf16[2048,8]{0,1:T(8,128)(2,1)} %param.27) | copy-start | bytes 98308
  30.3 15.2 %copy-start.3 = (bf16[1,16,2048]{2,1,0:T(8,128)(2,1)S(1)}, bf16[1,16,2048]{2,1,0:T(8,128)(2,1)}, u32[]{:S(2)}) copy-start(bf16[1,16,2048]{2,1,0:T(8,128)(2,1)} %residual_ref.5) | copy-start | bytes 196612
  30.3 15.2 %copy-start.10 = (s32[16,2]{0,1:T(2,128)S(1)}, s32[16,2]{0,1:T(2,128)}, u32[]{:S(2)}) copy-start(s32[16,2]{0,1:T(2,128)} %param.25) | copy-start | bytes 388
  30.3 45.8 %copy-start.2 = (bf16[176,2048]{1,0:T(8,128)(2,1)S(1)}, bf16[176,2048]{1,0:T(8,128)(2,1)}, u32[]{:S(2)}) copy-start(bf16[176,2048]{1,0:T(8,128)(2,1)} %down_ref.1) | copy-start | bytes 2162692
  30.7 45.5 %copy-start = (bf16[176,2048]{1,0:T(8,128)(2,1)S(1)}, bf16[176,2048]{1,0:T(8,128)(2,1)}, u32[]{:S(2)}) copy-start(bf16[176,2048]{1,0:T(8,128)(2,1)} %gate_ref.1) | copy-start | bytes 2162692
  30.7 45.5 %copy-start.1 = (bf16[176,2048]{1,0:T(8,128)(2,1)S(1)}, bf16[176,2048]{1,0:T(8,128)(2,1)}, u32[]{:S(2)}) copy-start(bf16[176,2048]{1,0:T(8,128)(2,1)} %up_ref.1) | copy-start | bytes 2162692
  65.5 10.6 %copy-start.6 = (bf16[2048,8]{0,1:T(8,128)(2,1)S(1)}, bf16[2048,8]{0,1:T(8,128)(2,1)}, u32[]{:S(2)}) copy-start(bf16[2048,8]{0,1:T(8,128)(2,1)} %param.28) | copy-start | bytes 98308
  77.0 41.9 %copy-start.4 = (bf16[125,2048]{1,0:T(8,128)(2,1)S(1)}, bf16[125,2048]{1,0:T(8,128)(2,1)}, u32[]{:S(2)}) copy-start(bf16[125,2048]{1,0:T(8,128)(2,1)} %words_ref.1) | copy-start | bytes 1536004

commit v7 on v6

--- a/solution.py
+++ b/solution.py
@@ -285,14 +285,15 @@
     sources = in_ref.shape[0]
     expert = expert_of_plane()
     for source in range(sources):
-        stats_ref[source] = in_ref[source, head_rows : head_rows + 8, :].astype(F32)
-        weight_ref[source * weight_rows : (source + 1) * weight_rows, :] = in_ref[
+        place = source % columns * groups + source // columns
+        stats_ref[place] = in_ref[source, head_rows : head_rows + 8, :].astype(F32)
+        weight_ref[place * weight_rows : (place + 1) * weight_rows, :] = in_ref[
             source, head_rows + 8 :, :
         ]
     stats = stats_ref[...].reshape(columns, groups, 8, LANES)
 
     def part(n, g):
-        source = n * groups + g
+        source = g * columns + n
         return jnp.concatenate(
             [in_ref[source, j * 8 : (j + 1) * 8, :] for j in range(HEADS_ROW)], axis=1
         ).astype(F32)
@@ -361,7 +362,7 @@
         total = total + attention_ref[n].astype(F32)
     for n in range(in_ref.shape[0]):
         total = total + in_ref[n].astype(F32)
-    chunk = lax.axis_index("x") * lax.axis_size("req") + lax.axis_index("req")
+    chunk = lax.axis_index("req") * lax.axis_size("x") + lax.axis_index("x")
     at = pl.ds(pl.multiple_of(chunk * LANES, LANES), LANES)
     total = (total + residual_ref[0, :, at].astype(F32)).astype(out_ref.dtype)
     half = out_ref.shape[1]
@@ -417,7 +418,7 @@
     guidance,
 ):
     planes = lax.axis_size("z")
-    plane = ("x", "req")
+    plane = ("req", "x")
     members = lax.axis_size(plane)
     requests = residual.shape[1]
     shape = jax.ShapeDtypeStruct

time: 120 us -> 120 us (level)
  no operation moved by 1% of the time
where the time goes in v7:
time: 120 us; the launch traced here: 119 us
  blocking collectives  114 us (95%)
  Pallas kernels  5.03 us (4%)
    all_to_all x7, blocking collectives, exchanged(): return lax.all_to_all(value, axis, 0, 0, tiled=True)  114 us

profile of v7, /device:TPU:1, one launch (start us, length us, event | category | flops | bytes accessed | tf_op | source)
XLA Modules:
  0.0 119.2 jit_solution(14624725875397287210)
XLA Ops:
  0.0 2.3 %shard_map.181 = (bf16[16,8,640]{2,1,0:T(8,128)(2,1)S(1)}, f32[8,128]{1,0:T(8,128)S(1)}, s32[2,16]{1,0:T(2,128)S(1)}) custom-call(bf16[1,4,4096]{2,1,0:T(4,128)(2,1)} %q_hbm.1, bf16[1,4,48,2048]{3,2,1,0:T(8,128)(2,1)} %k_hbm.1, bf16[1,4,48,2048]{3,2,1,0:T(8,128)(2,1)} %v_hbm.1, bf16[1,4,2,2048]{3,2,1,0:T(2,128)(2,1)} %new_hbm.1, s32[1,4]{1,0:T(1,128)} %lengths_hbm.1, ...), custom_call_target="tpu_custom_call" | custom-call | tf_op jit(solution)/shard_map/pallas_call | solution.py:427
  2.4 0.0 copy-start.5
  2.4 0.0 copy-start.8
  2.4 0.0 copy-start.9
  2.4 0.0 copy-start.7
  2.4 27.9 %all_to_all.35.in_ref = bf16[16,8,640]{2,1,0:T(8,128)(2,1)S(1)} all-to-all(bf16[16,8,640]{2,1,0:T(8,128)(2,1)S(1)} %get-tuple-element.10), channel_id=1, replica_groups=mesh['cfg'=2,'z'=16,'x'=4,'req'=4] {'z'}, dimensions={0} | all-to-all | bytes 327680 | tf_op jit(solution)/shard_map/all_to_all | solution.py:396
  30.3 0.0 copy-done.8
  30.3 0.0 copy-start.3
  30.3 0.0 copy-start.10
  30.3 0.0 copy-start.2
  30.4 0.3 shard_map.182
  30.7 0.0 copy-start
  30.7 0.0 copy-start.1
  30.7 15.1 %all_to_all.36.in_ref = bf16[16,104,128]{2,1,0:T(8,128)(2,1)S(1)} all-to-all(bf16[16,104,128]{2,1,0:T(8,128)(2,1)S(1)} %get-tuple-element.11), channel_id=1, replica_groups=mesh['cfg'=2,'z'=16,'x'=4,'req'=4] {'req','x'}, dimensions={0} | all-to-all | bytes 851968 | tf_op jit(solution)/shard_map/all_to_all | solution.py:396
  45.8 0.6 shard_map.183
  46.4 20.2 %all_to_all.37.in_ref.attention_ref = bf16[16,16,128]{2,1,0:T(8,128)(2,1)S(1)} all-to-all(bf16[16,16,128]{2,1,0:T(8,128)(2,1)S(1)} %shard_map.183), channel_id=1, replica_groups=mesh['cfg'=2,'z'=16,'x'=4,'req'=4] {'z'}, dimensions={0} | all-to-all | bytes 131072 | tf_op jit(solution)/shard_map/all_to_all | solution.py:396
  66.6 9.4 %all_to_all.38.in_ref = bf16[16,16,128]{2,1,0:T(8,128)(2,1)S(1)} all-to-all(bf16[16,16,128]{2,1,0:T(8,128)(2,1)S(1)} %shard_map.184), channel_id=1, replica_groups=mesh['cfg'=2,'z'=16,'x'=4,'req'=4] {'req','x'}, dimensions={0} | all-to-all | bytes 131072 | tf_op jit(solution)/shard_map/all_to_all | solution.py:396
  76.1 0.0 copy-done.6
  76.1 0.8 shard_map.185
  76.9 9.5 %all_to_all.39.in_ref = bf16[16,16,128]{2,1,0:T(8,128)(2,1)S(1)} all-to-all(bf16[16,16,128]{2,1,0:T(8,128)(2,1)S(1)} %shard_map.185), channel_id=1, replica_groups=mesh['cfg'=2,'z'=16,'x'=4,'req'=4] {'req','x'}, dimensions={0} | all-to-all | bytes 131072 | tf_op jit(solution)/shard_map/all_to_all | solution.py:396
  86.5 14.4 %all_to_all.40.in_ref = bf16[16,16,128]{2,1,0:T(8,128)(2,1)S(1)} all-to-all(bf16[16,16,128]{2,1,0:T(8,128)(2,1)S(1)} %shard_map.186), channel_id=1, replica_groups=mesh['cfg'=2,'z'=16,'x'=4,'req'=4] {'z'}, dimensions={0} | all-to-all | bytes 131072 | tf_op jit(solution)/shard_map/all_to_all | solution.py:396
  100.9 17.4 %all_to_all.41.in_ref = bf16[32,8,128]{2,1,0:T(8,128)(2,1)S(1)} all-to-all(bf16[32,8,128]{2,1,0:T(8,128)(2,1)S(1)} %shard_map.187), channel_id=1, replica_groups=mesh['cfg'=2,'z'=16,'x'=4,'req'=4] {'cfg','req','x'}, dimensions={0} | all-to-all | bytes 131072 | tf_op jit(solution)/shard_map/all_to_all | solution.py:396
  118.3 0.0 copy-done.4
  118.3 0.9 shard_map.188
  (13 shorter events, 0.1 us)
Async XLA Ops:
  2.4 28.0 %copy-start.5 = (bf16[64,2048]{1,0:T(8,128)(2,1)S(1)}, bf16[64,2048]{1,0:T(8,128)(2,1)}, u32[]{:S(2)}) copy-start(bf16[64,2048]{1,0:T(8,128)(2,1)} %weight_ref.1) | copy-start | bytes 786436
  2.4 27.9 %copy-start.8 = (bf16[2048]{0:T(1024)(128)(2,1)S(1)}, bf16[2048]{0:T(1024)(128)(2,1)}, u32[]{:S(2)}) copy-start(bf16[2048]{0:T(1024)(128)(2,1)} %first_gain_ref.1) | copy-start | bytes 12292
  2.4 27.9 %copy-start.9 = (bf16[2048]{0:T(1024)(128)(2,1)S(1)}, bf16[2048]{0:T(1024)(128)(2,1)}, u32[]{:S(2)}) copy-start(bf16[2048]{0:T(1024)(128)(2,1)} %second_gain_ref.1) | copy-start | bytes 12292
  2.4 43.4 %copy-start.7 = (bf16[2048,8]{0,1:T(8,128)(2,1)S(1)}, bf16[2048,8]{0,1:T(8,128)(2,1)}, u32[]{:S(2)}) copy-start(bf16[2048,8]{0,1:T(8,128)(2,1)} %param.27) | copy-start | bytes 98308
  30.3 15.5 %copy-start.3 = (bf16[1,16,2048]{2,1,0:T(8,128)(2,1)S(1)}, bf16[1,16,2048]{2,1,0:T(8,128)(2,1)}, u32[]{:S(2)}) copy-start(bf16[1,16,2048]{2,1,0:T(8,128)(2,1)} %residual_ref.5) | copy-start | bytes 196612
  30.3 15.5 %copy-start.10 = (s32[16,2]{0,1:T(2,128)S(1)}, s32[16,2]{0,1:T(2,128)}, u32[]{:S(2)}) copy-start(s32[16,2]{0,1:T(2,128)} %param.25) | copy-start | bytes 388
  30.3 45.7 %copy-start.2 = (bf16[176,2048]{1,0:T(8,128)(2,1)S(1)}, bf16[176,2048]{1,0:T(8,128)(2,1)}, u32[]{:S(2)}) copy-start(bf16[176,2048]{1,0:T(8,128)(2,1)} %down_ref.1) | copy-start | bytes 2162692
  30.7 45.4 %copy-start = (bf16[176,2048]{1,0:T(8,128)(2,1)S(1)}, bf16[176,2048]{1,0:T(8,128)(2,1)}, u32[]{:S(2)}) copy-start(bf16[176,2048]{1,0:T(8,128)(2,1)} %gate_ref.1) | copy-start | bytes 2162692
  30.7 45.4 %copy-start.1 = (bf16[176,2048]{1,0:T(8,128)(2,1)S(1)}, bf16[176,2048]{1,0:T(8,128)(2,1)}, u32[]{:S(2)}) copy-start(bf16[176,2048]{1,0:T(8,128)(2,1)} %up_ref.1) | copy-start | bytes 2162692
  66.6 9.4 %copy-start.6 = (bf16[2048,8]{0,1:T(8,128)(2,1)S(1)}, bf16[2048,8]{0,1:T(8,128)(2,1)}, u32[]{:S(2)}) copy-start(bf16[2048,8]{0,1:T(8,128)(2,1)} %param.28) | copy-start | bytes 98308
  76.9 41.4 %copy-start.4 = (bf16[125,2048]{1,0:T(8,128)(2,1)S(1)}, bf16[125,2048]{1,0:T(8,128)(2,1)}, u32[]{:S(2)}) copy-start(bf16[125,2048]{1,0:T(8,128)(2,1)} %words_ref.1) | copy-start | bytes 1536004

commit v8 on v7

--- a/solution.py
+++ b/solution.py
@@ -369,7 +369,7 @@
     copies = out_ref.shape[0] // 2
     for stream in range(2):
         for copy in range(copies):
-            out_ref[stream * copies + copy] = total[stream * half : (stream + 1) * half]
+            out_ref[copy * 2 + stream] = total[stream * half : (stream + 1) * half]
 
 
 def head_kernel(in_ref, gain_ref, words_ref, factor_ref, out_ref):
@@ -378,7 +378,7 @@
     joined = jnp.concatenate(
         [
             jnp.concatenate(
-                [in_ref[stream * chunks + chunk].astype(F32) for chunk in range(chunks)], axis=1
+                [in_ref[chunk * 2 + stream].astype(F32) for chunk in range(chunks)], axis=1
             )
             for stream in range(2)
         ],
@@ -503,7 +503,7 @@
     final = call(
         finish_kernel, shape((streams * members, requests // 2, LANES), BF16), [vmem()] * 3
     )(hidden, projected, residual)
-    final = exchanged(final, ("cfg",) + plane)
+    final = exchanged(final, plane + ("cfg",))
 
     return call(
         head_kernel,

time: 120 us -> 120 us (level)
  no operation moved by 1% of the time
where the time goes in v8:
time: 120 us; the launch traced here: 119 us
  blocking collectives  114 us (95%)
  Pallas kernels  5.04 us (4%)
    all_to_all x7, blocking collectives, exchanged(): return lax.all_to_all(value, axis, 0, 0, tiled=True)  114 us

profile of v8, /device:TPU:1, one launch (start us, length us, event | category | flops | bytes accessed | tf_op | source)
XLA Modules:
  0.0 119.4 jit_solution(2812169537121030327)
XLA Ops:
  0.0 2.3 %shard_map.181 = (bf16[16,8,640]{2,1,0:T(8,128)(2,1)S(1)}, f32[8,128]{1,0:T(8,128)S(1)}, s32[2,16]{1,0:T(2,128)S(1)}) custom-call(bf16[1,4,4096]{2,1,0:T(4,128)(2,1)} %q_hbm.1, bf16[1,4,48,2048]{3,2,1,0:T(8,128)(2,1)} %k_hbm.1, bf16[1,4,48,2048]{3,2,1,0:T(8,128)(2,1)} %v_hbm.1, bf16[1,4,2,2048]{3,2,1,0:T(2,128)(2,1)} %new_hbm.1, s32[1,4]{1,0:T(1,128)} %lengths_hbm.1, ...), custom_call_target="tpu_custom_call" | custom-call | tf_op jit(solution)/shard_map/pallas_call | solution.py:427
  2.4 0.0 copy-start.5
  2.4 0.0 copy-start.8
  2.4 0.0 copy-start.9
  2.4 0.0 copy-start.7
  2.4 27.9 %all_to_all.35.in_ref = bf16[16,8,640]{2,1,0:T(8,128)(2,1)S(1)} all-to-all(bf16[16,8,640]{2,1,0:T(8,128)(2,1)S(1)} %get-tuple-element.10), channel_id=1, replica_groups=mesh['cfg'=2,'z'=16,'x'=4,'req'=4] {'z'}, dimensions={0} | all-to-all | bytes 327680 | tf_op jit(solution)/shard_map/all_to_all | solution.py:396
  30.3 0.0 copy-done.9
  30.3 0.0 copy-start.3
  30.3 0.0 copy-start.10
  30.3 0.0 copy-start.2
  30.4 0.3 shard_map.182
  30.7 0.0 copy-start
  30.7 0.0 copy-start.1
  30.7 15.1 %all_to_all.36.in_ref = bf16[16,104,128]{2,1,0:T(8,128)(2,1)S(1)} all-to-all(bf16[16,104,128]{2,1,0:T(8,128)(2,1)S(1)} %get-tuple-element.11), channel_id=1, replica_groups=mesh['cfg'=2,'z'=16,'x'=4,'req'=4] {'req','x'}, dimensions={0} | all-to-all | bytes 851968 | tf_op jit(solution)/shard_map/all_to_all | solution.py:396
  45.8 0.0 copy-done.7
  45.8 0.6 shard_map.183
  46.4 20.2 %all_to_all.37.in_ref.attention_ref = bf16[16,16,128]{2,1,0:T(8,128)(2,1)S(1)} all-to-all(bf16[16,16,128]{2,1,0:T(8,128)(2,1)S(1)} %shard_map.183), channel_id=1, replica_groups=mesh['cfg'=2,'z'=16,'x'=4,'req'=4] {'z'}, dimensions={0} | all-to-all | bytes 131072 | tf_op jit(solution)/shard_map/all_to_all | solution.py:396
  66.6 9.4 %all_to_all.38.in_ref = bf16[16,16,128]{2,1,0:T(8,128)(2,1)S(1)} all-to-all(bf16[16,16,128]{2,1,0:T(8,128)(2,1)S(1)} %shard_map.184), channel_id=1, replica_groups=mesh['cfg'=2,'z'=16,'x'=4,'req'=4] {'req','x'}, dimensions={0} | all-to-all | bytes 131072 | tf_op jit(solution)/shard_map/all_to_all | solution.py:396
  76.1 0.0 copy-done.2
  76.1 0.8 shard_map.185
  76.9 9.5 %all_to_all.39.in_ref = bf16[16,16,128]{2,1,0:T(8,128)(2,1)S(1)} all-to-all(bf16[16,16,128]{2,1,0:T(8,128)(2,1)S(1)} %shard_map.185), channel_id=1, replica_groups=mesh['cfg'=2,'z'=16,'x'=4,'req'=4] {'req','x'}, dimensions={0} | all-to-all | bytes 131072 | tf_op jit(solution)/shard_map/all_to_all | solution.py:396
  86.5 14.4 %all_to_all.40.in_ref = bf16[16,16,128]{2,1,0:T(8,128)(2,1)S(1)} all-to-all(bf16[16,16,128]{2,1,0:T(8,128)(2,1)S(1)} %shard_map.186), channel_id=1, replica_groups=mesh['cfg'=2,'z'=16,'x'=4,'req'=4] {'z'}, dimensions={0} | all-to-all | bytes 131072 | tf_op jit(solution)/shard_map/all_to_all | solution.py:396
  100.9 17.6 %all_to_all.41.in_ref = bf16[32,8,128]{2,1,0:T(8,128)(2,1)S(1)} all-to-all(bf16[32,8,128]{2,1,0:T(8,128)(2,1)S(1)} %shard_map.187), channel_id=1, replica_groups=mesh['cfg'=2,'z'=16,'x'=4,'req'=4] {'req','x','cfg'}, dimensions={0} | all-to-all | bytes 131072 | tf_op jit(solution)/shard_map/all_to_all | solution.py:396
  118.5 0.9 shard_map.188
  (13 shorter events, 0.1 us)
Async XLA Ops:
  2.4 28.0 %copy-start.5 = (bf16[64,2048]{1,0:T(8,128)(2,1)S(1)}, bf16[64,2048]{1,0:T(8,128)(2,1)}, u32[]{:S(2)}) copy-start(bf16[64,2048]{1,0:T(8,128)(2,1)} %weight_ref.1) | copy-start | bytes 786436
  2.4 27.9 %copy-start.8 = (bf16[2048]{0:T(1024)(128)(2,1)S(1)}, bf16[2048]{0:T(1024)(128)(2,1)}, u32[]{:S(2)}) copy-start(bf16[2048]{0:T(1024)(128)(2,1)} %first_gain_ref.1) | copy-start | bytes 12292
  2.4 27.9 %copy-start.9 = (bf16[2048]{0:T(1024)(128)(2,1)S(1)}, bf16[2048]{0:T(1024)(128)(2,1)}, u32[]{:S(2)}) copy-start(bf16[2048]{0:T(1024)(128)(2,1)} %second_gain_ref.1) | copy-start | bytes 12292
  2.4 43.4 %copy-start.7 = (bf16[2048,8]{0,1:T(8,128)(2,1)S(1)}, bf16[2048,8]{0,1:T(8,128)(2,1)}, u32[]{:S(2)}) copy-start(bf16[2048,8]{0,1:T(8,128)(2,1)} %param.27) | copy-start | bytes 98308
  30.3 15.5 %copy-start.3 = (bf16[1,16,2048]{2,1,0:T(8,128)(2,1)S(1)}, bf16[1,16,2048]{2,1,0:T(8,128)(2,1)}, u32[]{:S(2)}) copy-start(bf16[1,16,2048]{2,1,0:T(8,128)(2,1)} %residual_ref.5) | copy-start | bytes 196612
  30.3 15.5 %copy-start.10 = (s32[16,2]{0,1:T(2,128)S(1)}, s32[16,2]{0,1:T(2,128)}, u32[]{:S(2)}) copy-start(s32[16,2]{0,1:T(2,128)} %param.25) | copy-start | bytes 388
  30.3 45.7 %copy-start.2 = (bf16[176,2048]{1,0:T(8,128)(2,1)S(1)}, bf16[176,2048]{1,0:T(8,128)(2,1)}, u32[]{:S(2)}) copy-start(bf16[176,2048]{1,0:T(8,128)(2,1)} %down_ref.1) | copy-start | bytes 2162692
  30.7 45.4 %copy-start = (bf16[176,2048]{1,0:T(8,128)(2,1)S(1)}, bf16[176,2048]{1,0:T(8,128)(2,1)}, u32[]{:S(2)}) copy-start(bf16[176,2048]{1,0:T(8,128)(2,1)} %gate_ref.1) | copy-start | bytes 2162692
  30.7 45.4 %copy-start.1 = (bf16[176,2048]{1,0:T(8,128)(2,1)S(1)}, bf16[176,2048]{1,0:T(8,128)(2,1)}, u32[]{:S(2)}) copy-start(bf16[176,2048]{1,0:T(8,128)(2,1)} %up_ref.1) | copy-start | bytes 2162692
  66.6 9.4 %copy-start.6 = (bf16[2048,8]{0,1:T(8,128)(2,1)S(1)}, bf16[2048,8]{0,1:T(8,128)(2,1)}, u32[]{:S(2)}) copy-start(bf16[2048,8]{0,1:T(8,128)(2,1)} %param.28) | copy-start | bytes 98308
  76.9 41.6 %copy-start.4 = (bf16[125,2048]{1,0:T(8,128)(2,1)S(1)}, bf16[125,2048]{1,0:T(8,128)(2,1)}, u32[]{:S(2)}) copy-start(bf16[125,2048]{1,0:T(8,128)(2,1)} %words_ref.1) | copy-start | bytes 1536004

commit v9 on v8

--- a/solution.py
+++ b/solution.py
@@ -307,11 +307,13 @@
     attended = jnp.concatenate(
         [top / jnp.maximum(bottom, 1e-30) for top, bottom in zip(numerator, denominator)], axis=0
     )
-    gated = (attended.astype(BF16).astype(F32) * gate).astype(BF16)
-    wide = HEADS_ROW * HD
-    lower = dot(gated, weight_ref[:wide, :])
-    upper = dot(gated, weight_ref[wide:, :])
-    mixed = jnp.where(row % 8 < requests, lower, upper)
+    gated = (attended.astype(BF16).astype(F32) * gate).astype(BF16).astype(F32)
+    low_heads = row % 8 < requests
+    none = jnp.zeros_like(gated)
+    both_halves = jnp.concatenate(
+        [jnp.where(low_heads, gated, none), jnp.where(low_heads, none, gated)], axis=1
+    )
+    mixed = dot(both_halves.astype(BF16), weight_ref[...])
     sub = iota((8, LANES), 0)
     tiles = []
     for g in range(groups):

time: 120 us -> 120 us (level)
  no operation moved by 1% of the time
where the time goes in v9:
time: 120 us; the launch traced here: 119 us
  blocking collectives  114 us (95%)
  Pallas kernels  5.04 us (4%)
    all_to_all x7, blocking collectives, exchanged(): return lax.all_to_all(value, axis, 0, 0, tiled=True)  114 us

profile of v9, /device:TPU:1, one launch (start us, length us, event | category | flops | bytes accessed | tf_op | source)
XLA Modules:
  0.0 119.4 jit_solution(388742955224869013)
XLA Ops:
  0.0 2.3 %shard_map.181 = (bf16[16,8,640]{2,1,0:T(8,128)(2,1)S(1)}, f32[8,128]{1,0:T(8,128)S(1)}, s32[2,16]{1,0:T(2,128)S(1)}) custom-call(bf16[1,4,4096]{2,1,0:T(4,128)(2,1)} %q_hbm.1, bf16[1,4,48,2048]{3,2,1,0:T(8,128)(2,1)} %k_hbm.1, bf16[1,4,48,2048]{3,2,1,0:T(8,128)(2,1)} %v_hbm.1, bf16[1,4,2,2048]{3,2,1,0:T(2,128)(2,1)} %new_hbm.1, s32[1,4]{1,0:T(1,128)} %lengths_hbm.1, ...), custom_call_target="tpu_custom_call" | custom-call | tf_op jit(solution)/shard_map/pallas_call | solution.py:429
  2.4 0.0 copy-start.5
  2.4 0.0 copy-start.8
  2.4 0.0 copy-start.9
  2.4 0.0 copy-start.7
  2.4 27.9 %all_to_all.35.in_ref = bf16[16,8,640]{2,1,0:T(8,128)(2,1)S(1)} all-to-all(bf16[16,8,640]{2,1,0:T(8,128)(2,1)S(1)} %get-tuple-element.10), channel_id=1, replica_groups=mesh['cfg'=2,'z'=16,'x'=4,'req'=4] {'z'}, dimensions={0} | all-to-all | bytes 327680 | tf_op jit(solution)/shard_map/all_to_all | solution.py:398
  30.3 0.0 copy-done.9
  30.3 0.0 copy-start.3
  30.3 0.0 copy-start.10
  30.3 0.0 copy-start.2
  30.4 0.3 shard_map.182
  30.7 0.0 copy-start
  30.7 0.0 copy-start.1
  30.7 15.1 %all_to_all.36.in_ref = bf16[16,104,128]{2,1,0:T(8,128)(2,1)S(1)} all-to-all(bf16[16,104,128]{2,1,0:T(8,128)(2,1)S(1)} %get-tuple-element.11), channel_id=1, replica_groups=mesh['cfg'=2,'z'=16,'x'=4,'req'=4] {'req','x'}, dimensions={0} | all-to-all | bytes 851968 | tf_op jit(solution)/shard_map/all_to_all | solution.py:398
  45.8 0.0 copy-done.7
  45.8 0.6 shard_map.183
  46.4 20.2 %all_to_all.37.in_ref.attention_ref = bf16[16,16,128]{2,1,0:T(8,128)(2,1)S(1)} all-to-all(bf16[16,16,128]{2,1,0:T(8,128)(2,1)S(1)} %shard_map.183), channel_id=1, replica_groups=mesh['cfg'=2,'z'=16,'x'=4,'req'=4] {'z'}, dimensions={0} | all-to-all | bytes 131072 | tf_op jit(solution)/shard_map/all_to_all | solution.py:398
  66.6 9.4 %all_to_all.38.in_ref = bf16[16,16,128]{2,1,0:T(8,128)(2,1)S(1)} all-to-all(bf16[16,16,128]{2,1,0:T(8,128)(2,1)S(1)} %shard_map.184), channel_id=1, replica_groups=mesh['cfg'=2,'z'=16,'x'=4,'req'=4] {'req','x'}, dimensions={0} | all-to-all | bytes 131072 | tf_op jit(solution)/shard_map/all_to_all | solution.py:398
  76.1 0.0 copy-done
  76.1 0.8 shard_map.185
  76.9 9.5 %all_to_all.39.in_ref = bf16[16,16,128]{2,1,0:T(8,128)(2,1)S(1)} all-to-all(bf16[16,16,128]{2,1,0:T(8,128)(2,1)S(1)} %shard_map.185), channel_id=1, replica_groups=mesh['cfg'=2,'z'=16,'x'=4,'req'=4] {'req','x'}, dimensions={0} | all-to-all | bytes 131072 | tf_op jit(solution)/shard_map/all_to_all | solution.py:398
  86.5 14.4 %all_to_all.40.in_ref = bf16[16,16,128]{2,1,0:T(8,128)(2,1)S(1)} all-to-all(bf16[16,16,128]{2,1,0:T(8,128)(2,1)S(1)} %shard_map.186), channel_id=1, replica_groups=mesh['cfg'=2,'z'=16,'x'=4,'req'=4] {'z'}, dimensions={0} | all-to-all | bytes 131072 | tf_op jit(solution)/shard_map/all_to_all | solution.py:398
  100.9 17.6 %all_to_all.41.in_ref = bf16[32,8,128]{2,1,0:T(8,128)(2,1)S(1)} all-to-all(bf16[32,8,128]{2,1,0:T(8,128)(2,1)S(1)} %shard_map.187), channel_id=1, replica_groups=mesh['cfg'=2,'z'=16,'x'=4,'req'=4] {'req','x','cfg'}, dimensions={0} | all-to-all | bytes 131072 | tf_op jit(solution)/shard_map/all_to_all | solution.py:398
  118.5 0.9 shard_map.188
  (13 shorter events, 0.1 us)
Async XLA Ops:
  2.4 28.0 %copy-start.5 = (bf16[64,2048]{1,0:T(8,128)(2,1)S(1)}, bf16[64,2048]{1,0:T(8,128)(2,1)}, u32[]{:S(2)}) copy-start(bf16[64,2048]{1,0:T(8,128)(2,1)} %weight_ref.1) | copy-start | bytes 786436
  2.4 27.9 %copy-start.8 = (bf16[2048]{0:T(1024)(128)(2,1)S(1)}, bf16[2048]{0:T(1024)(128)(2,1)}, u32[]{:S(2)}) copy-start(bf16[2048]{0:T(1024)(128)(2,1)} %first_gain_ref.1) | copy-start | bytes 12292
  2.4 27.9 %copy-start.9 = (bf16[2048]{0:T(1024)(128)(2,1)S(1)}, bf16[2048]{0:T(1024)(128)(2,1)}, u32[]{:S(2)}) copy-start(bf16[2048]{0:T(1024)(128)(2,1)} %second_gain_ref.1) | copy-start | bytes 12292
  2.4 43.4 %copy-start.7 = (bf16[2048,8]{0,1:T(8,128)(2,1)S(1)}, bf16[2048,8]{0,1:T(8,128)(2,1)}, u32[]{:S(2)}) copy-start(bf16[2048,8]{0,1:T(8,128)(2,1)} %param.27) | copy-start | bytes 98308
  30.3 15.5 %copy-start.3 = (bf16[1,16,2048]{2,1,0:T(8,128)(2,1)S(1)}, bf16[1,16,2048]{2,1,0:T(8,128)(2,1)}, u32[]{:S(2)}) copy-start(bf16[1,16,2048]{2,1,0:T(8,128)(2,1)} %residual_ref.5) | copy-start | bytes 196612
  30.3 15.5 %copy-start.10 = (s32[16,2]{0,1:T(2,128)S(1)}, s32[16,2]{0,1:T(2,128)}, u32[]{:S(2)}) copy-start(s32[16,2]{0,1:T(2,128)} %param.25) | copy-start | bytes 388
  30.3 45.7 %copy-start.2 = (bf16[176,2048]{1,0:T(8,128)(2,1)S(1)}, bf16[176,2048]{1,0:T(8,128)(2,1)}, u32[]{:S(2)}) copy-start(bf16[176,2048]{1,0:T(8,128)(2,1)} %down_ref.1) | copy-start | bytes 2162692
  30.7 45.4 %copy-start = (bf16[176,2048]{1,0:T(8,128)(2,1)S(1)}, bf16[176,2048]{1,0:T(8,128)(2,1)}, u32[]{:S(2)}) copy-start(bf16[176,2048]{1,0:T(8,128)(2,1)} %gate_ref.1) | copy-start | bytes 2162692
  30.7 45.4 %copy-start.1 = (bf16[176,2048]{1,0:T(8,128)(2,1)S(1)}, bf16[176,2048]{1,0:T(8,128)(2,1)}, u32[]{:S(2)}) copy-start(bf16[176,2048]{1,0:T(8,128)(2,1)} %up_ref.1) | copy-start | bytes 2162692
  66.6 9.4 %copy-start.6 = (bf16[2048,8]{0,1:T(8,128)(2,1)S(1)}, bf16[2048,8]{0,1:T(8,128)(2,1)}, u32[]{:S(2)}) copy-start(bf16[2048,8]{0,1:T(8,128)(2,1)} %param.28) | copy-start | bytes 98308
  76.9 41.6 %copy-start.4 = (bf16[125,2048]{1,0:T(8,128)(2,1)S(1)}, bf16[125,2048]{1,0:T(8,128)(2,1)}, u32[]{:S(2)}) copy-start(bf16[125,2048]{1,0:T(8,128)(2,1)} %words_ref.1) | copy-start | bytes 1536004
